TPU v7x, 512 devices: a whole 4x8x8 slice. The times are simulated.
512 devices in a mesh: bins: 32 (over z, x), xy: 16 (over y, core).
Axes of the slice: x: 4, y: 8, z: 8, core: 2. Of those that a mesh axis runs over, the one named last changes fastest.
Arguments:
- conc: float32 [32, 128, 64, 256], P('bins', None, 'xy'), may hold values from 0.05 to 2
- vel_x: float32 [32, 64, 256], P('bins', 'xy'), may hold values from -0.3 to 0.3
- vel_y: float32 [32, 64, 256], P('bins', 'xy'), may hold values from -0.3 to 0.3
- sea_mask: int32 [64, 256], P('xy'), may hold values 0 or 1
- settle: float32 [128], replicated, may hold values from 0.05 to 0.6
- size_bin_kernel_class: int32 [128], replicated, may hold values from 0 to 7
- aggregate_upward_factor: float32 [8], replicated, may hold values from 0.25 to 2
- agg_down: float32 [8], replicated, may hold values from 0.25 to 2
- break_rate: float32 [8], replicated, may hold values from 0.05 to 0.5
Outputs:
- conc_next: float32 [32, 128, 64, 256], P('bins', None, 'xy')
All inputs are finite; a program needn't handle non-finite values. No bound on the sum of `sea_mask` on one device may be relied on, other than what follows from the above.
Results may differ from a plain program's by a relative error of at most 0.00007.
Values sent between devices are 32-bit elements; how exact they have to be, the bound alone decides.
A program may use at most 64 MiB of HBM per device.

v0:
```python
import jax
import jax.numpy as jnp
from jax import lax
from jax.sharding import PartitionSpec as P

NB = 128
NCLS = 8
HSUB = 2
VERTICAL_SUBSTEP = 2


h_diffusion = 0.2
v_diffusion = 0.2
step_duration = 0.5
collide_scale = 2.0


def extended(cells, sides, width):
    for axis, dim in sides:
        count = lax.axis_size(axis)
        ends = count - 1
        head = lax.slice_in_dim(cells, 0, width, axis=dim)
        tail = lax.slice_in_dim(cells, cells.shape[dim] - width, cells.shape[dim], axis=dim)
        cells = jnp.concatenate(
            [
                lax.ppermute(tail, axis, [(i, (i + 1) % count) for i in range(ends)]),
                cells,
                lax.ppermute(head, axis, [((i + 1) % count, i) for i in range(ends)]),
            ],
            axis=dim,
        )
    return cells


def prefix(value, axis, join, neutral, backward):
    count, mine = (lax.axis_size(axis), lax.axis_index(axis))
    pieces = jax.tree.map(lambda part: lax.all_gather(part, axis), value)
    if backward:
        pieces = jax.tree.map(lambda part: part[::-1], pieces)
        mine = count - 1 - mine
    running = jax.tree.map(
        lambda part, zero: jnp.full_like(part, 0) + jnp.asarray(zero, part.dtype), value, neutral
    )

    def lap(position, running):
        longer = join(running, jax.tree.map(lambda part: part[position], pieces))
        return jax.tree.map(lambda new, old: jnp.where(position < mine, new, old), longer, running)

    return lax.fori_loop(0, count - 1, lap, running)


def add_parts(earlier, later):
    return jax.tree.map(jnp.add, earlier, later)


def settle_mix(column, sink):
    flux = sink * column
    above = jnp.concatenate([jnp.zeros_like(flux[:1]), flux[:-1]], 0)
    upper = jnp.concatenate([column[:1], column[:-1]], 0)
    lower = jnp.concatenate([column[1:], column[-1:]], 0)
    return column - flux + above + v_diffusion * (upper + lower - 2.0 * column)


def lookup(table, onehot):
    return jnp.dot(onehot, table, precision=lax.Precision.HIGHEST)[:, None, None]


def local(
    conc,
    vel_x,
    vel_y,
    sea_mask,
    settle,
    size_bin_kernel_class,
    aggregate_upward_factor,
    agg_down,
    break_rate,
):
    water = sea_mask.astype(jnp.float32)
    speed_x = vel_x[:, None]
    speed_y = vel_y[:, None]
    level = conc
    for unused_item in range(HSUB):
        padded = extended(level, (("xy", 2),), 1)
        east = padded[:, :, 2:, :]
        west = padded[:, :, :-2, :]
        side = jnp.pad(level, ((0, 0), (0, 0), (0, 0), (1, 1)))
        north = side[:, :, :, 2:]
        south = side[:, :, :, :-2]
        level = water * (
            level
            - 0.5 * speed_x * (east - west)
            - 0.5 * speed_y * (north - south)
            + h_diffusion * (east + west + north + south - 4.0 * level)
        )
    classes = jnp.arange(NCLS)
    count_bins = lax.axis_size("bins")
    local_size_bins = NB // count_bins
    first_bin = lax.axis_index("bins") * local_size_bins
    own_class = lax.dynamic_slice_in_dim(size_bin_kernel_class, first_bin, local_size_bins)
    onehot = (own_class[:, None] == classes[None, :]).astype(jnp.float32)
    sink = lax.dynamic_slice_in_dim(settle, first_bin, local_size_bins)[:, None, None]
    bin_index = first_bin + jnp.arange(local_size_bins)
    block = lax.all_to_all(level, "bins", split_axis=1, concat_axis=0, tiled=True)
    for unused_item in range(VERTICAL_SUBSTEP):
        block = settle_mix(block, sink)
    up_rate = lookup(aggregate_upward_factor, onehot)
    down_rate = lookup(agg_down, onehot)
    brk_rate = lookup(break_rate, onehot)
    weight = (1.0 / jnp.maximum(bin_index, 1).astype(jnp.float32))[:, None, None]
    broken = (bin_index >= 1).astype(jnp.float32)[:, None, None]
    up_terms = up_rate * block
    down_terms = down_rate * block
    fragmentation_terms = brk_rate * block * weight
    up_own = jnp.sum(up_terms, 1)
    down_own = jnp.sum(down_terms, 1)
    frag_own = jnp.sum(fragmentation_terms, 1)
    empty = jnp.zeros_like(up_own)
    up_lower = prefix(up_own, "bins", add_parts, empty, False)
    down_higher, frag_higher = prefix((down_own, frag_own), "bins", add_parts, (empty, empty), True)
    lower_sum = up_lower[:, None] + jnp.cumsum(up_terms, 1) - up_terms
    higher_sum = down_higher[:, None] + down_own[:, None] - jnp.cumsum(down_terms, 1)
    frag_sum = frag_higher[:, None] + frag_own[:, None] - jnp.cumsum(fragmentation_terms, 1)
    concentration_change = (
        collide_scale / NB * (down_rate * block * lower_sum - up_rate * block * higher_sum)
    )
    result = block + step_duration * (concentration_change + frag_sum - brk_rate * broken * block)
    result = lax.all_to_all(result, "bins", split_axis=0, concat_axis=1, tiled=True)
    return result


def solution(mesh):
    placed = (
        P("bins", None, "xy", None),
        P("bins", "xy", None),
        P("bins", "xy", None),
        P("xy", None),
        P(),
        P(),
        P(),
        P(),
        P(),
    )
    return jax.shard_map(
        local, mesh=mesh, in_specs=placed, out_specs=P("bins", None, "xy", None), check_vma=False
    )
```

profile of v0, /device:TPU:1, one launch (start us, length us, event | category | flops | bytes accessed | tf_op | source)
XLA Modules:
  0.0 382.0 jit_solution(12739953073839875429)
XLA Ops:
  6.5 1.5 fusion.34
  8.0 8.8 %collective-permute-start = (f32[1,128,1,256]{3,2,0,1:T(1,128)S(1)}, f32[1,128,1,256]{3,2,0,1:T(1,128)S(1)}, u32[]{:S(2)}, u32[]{:S(2)}) collective-permute-start(f32[1,128,1,256]{3,2,0,1:T(1,128)S(1)} %get-tuple-element.272), channel_id=1, source_target_pairs={{1,0},{2,1},{3,2},{4,3},{5,4},{6,5},{7,6},{8,7},{9,8},{10,9},{11,1... | collective-permute-start | bytes 393224 | tf_op jit(solution)/shard_map/ppermute | solution.py:28
  16.8 1.9 collective-permute-start.1
  20.7 3.5 add_multiply_fusion.1
  24.4 1.9 collective-permute-start.2
  26.3 4.4 %collective-permute-start.3 = (f32[1,128,1,256]{3,2,0,1:T(1,128)S(1)}, f32[1,128,1,256]{3,2,0,1:T(1,128)S(1)}, u32[]{:S(2)}, u32[]{:S(2)}) collective-permute-start(f32[1,128,1,256]{3,2,0,1:T(1,128)S(1)} %get-tuple-element.269), channel_id=1, source_target_pairs={{0,1},{1,2},{2,3},{3,4},{4,5},{5,6},{6,7},{7,8},{8,9},{9,10},{10,1... | collective-permute-start | bytes 393224 | tf_op jit(solution)/shard_map/ppermute | solution.py:26
  31.4 1.2 collective-permute-done.3
  32.6 2.3 add_multiply_fusion
  34.9 8.7 %all-to-all-start = ((f32[1,128,4,256]{3,2,0,1:T(4,128)}), f32[1,128,4,256]{3,2,0,1:T(4,128)S(1)}, u32[]{:S(2)}, u32[]{:S(2)}) async-start(f32[1,128,4,256]{3,2,0,1:T(4,128)} %add_multiply_fusion), calls=%async_computation | async-start | bytes 1048576 | tf_op jit(solution)/shard_map/all_to_all | solution.py:104
  44.5 15.2 %all-to-all-done = f32[1,128,4,256]{3,2,0,1:T(4,128)S(1)} async-done(((f32[1,128,4,256]{3,2,0,1:T(4,128)}), f32[1,128,4,256]{3,2,0,1:T(4,128)S(1)}, u32[]{:S(2)}, u32[]{:S(2)}) %all-to-all-start) | async-done | bytes 524320 | tf_op jit(solution)/shard_map/all_to_all | solution.py:104
  60.9 1.5 fusion.15
  64.0 82.0 %all-gather.9.cloned.1.call-done = f32[1024,4,256]{2,1,0:T(4,128)} async-done(((f32[32,4,256]{2,1,0:T(4,128)}), f32[1024,4,256]{2,1,0:T(4,128)}) %all-gather.9.cloned.1.call-update) | async-done | bytes 4194320 | tf_op jit(solution)/shard_map/all_gather | solution.py:37
  146.0 5.3 %rev.6 = f32[32,32,4,256]{3,2,1,0:T(4,128)} reverse(f32[32,32,4,256]{3,2,1,0:T(4,128)} %bitcast.51), dimensions={0} | reverse | bytes 8388608 | tf_op jit(solution)/shard_map/rev | solution.py:39
  151.3 82.6 %all-gather.11.cloned.1.call-done = f32[1024,4,256]{2,1,0:T(4,128)} async-done(((f32[32,4,256]{2,1,0:T(4,128)}), f32[1024,4,256]{2,1,0:T(4,128)}) %all-gather.11.cloned.1.call-update) | async-done | bytes 4194320 | tf_op jit(solution)/shard_map/all_gather | solution.py:37
  233.9 5.4 %rev.7 = f32[32,32,4,256]{3,2,1,0:T(4,128)} reverse(f32[32,32,4,256]{3,2,1,0:T(4,128)} %bitcast.52), dimensions={0} | reverse | bytes 8388608 | tf_op jit(solution)/shard_map/rev | solution.py:39
  239.3 35.2 %while.31 = (s32[]{:T(128)}, f32[32,4,256]{2,1,0:T(4,128)S(1)}, f32[32,4,256]{2,1,0:T(4,128)S(1)}, s32[]{:T(128)}, f32[32,32,4,256]{3,2,1,0:T(4,128)}, /*index=5*/f32[32,32,4,256]{3,2,1,0:T(4,128)}, s32[]{:T(128)}, s32[]{:T(128)}) while((s32[]{:T(128)}, f32[32,4,256]{2,1,0:T(4,128)S(1)}, f32[32,4,256]{2,1,0:T(4,128)S(1)}, ...), condition=%wide.region_7.8_spmd.clone, body=%wide.region_6.7_spmd.clone.sunk | while | flops 196612 | bytes 786541 | solution.py:49
  239.3 1.1 add_select_fusion.6
  240.5 1.1 add_select_fusion.6
  241.6 1.1 add_select_fusion.6
  242.7 1.1 add_select_fusion.6
  243.9 1.1 add_select_fusion.6
  245.0 1.1 add_select_fusion.6
  246.1 1.1 add_select_fusion.6
  247.3 1.1 add_select_fusion.6
  248.4 1.1 add_select_fusion.6
  249.5 1.1 add_select_fusion.6
  250.7 1.1 add_select_fusion.6
  251.8 1.1 add_select_fusion.6
  254.1 1.1 add_select_fusion.6
  255.2 1.1 add_select_fusion.6
  256.3 1.1 add_select_fusion.6
  257.5 1.1 add_select_fusion.6
  258.6 1.1 add_select_fusion.6
  259.7 1.1 add_select_fusion.6
  260.9 1.1 add_select_fusion.6
  262.0 1.1 add_select_fusion.6
  264.3 1.1 add_select_fusion.6
  265.4 1.1 add_select_fusion.6
  266.5 1.1 add_select_fusion.6
  267.7 1.1 add_select_fusion.6
  268.8 1.1 add_select_fusion.6
  269.9 1.1 add_select_fusion.6
  271.1 1.1 add_select_fusion.6
  272.2 1.1 add_select_fusion.6
  273.3 1.1 add_select_fusion.6
  274.6 47.3 %all-gather.7.cloned.1.call-done = f32[1024,4,256]{2,1,0:T(4,128)} async-done(((f32[32,4,256]{2,1,0:T(4,128)}), f32[1024,4,256]{2,1,0:T(4,128)}) %all-gather.7.cloned.1.call-update) | async-done | bytes 4194320 | tf_op jit(solution)/shard_map/all_gather | solution.py:37
  321.9 33.4 %while.30 = (s32[]{:T(128)}, f32[32,4,256]{2,1,0:T(4,128)S(1)}, s32[]{:T(128)}, f32[32,32,4,256]{3,2,1,0:T(4,128)}, s32[]{:T(128)}, /*index=5*/s32[]{:T(128)}) while((s32[]{:T(128)}, f32[32,4,256]{2,1,0:T(4,128)S(1)}, s32[]{:T(128)}, f32[32,32,4,256]{3,2,1,0:T(4,128)}, s32[]{:T(128)}, /*index=5*/s32[]{:T(128)}) %tuple.86), condition=%wide.region_2.3_spmd.clone, body=%wide.region_1.2_spmd.clone.sunk | while | flops 98308 | bytes 393309 | solution.py:49
  356.4 18.3 %all_to_all.24 = f32[32,4,4,256]{3,2,1,0:T(4,128)S(1)} all-to-all(f32[32,4,4,256]{3,2,1,0:T(4,128)S(1)} %fusion.8), channel_id=1, replica_groups=mesh['bins'=32,'xy'=16] {'bins'}, dimensions={0} | all-to-all | bytes 1048576 | tf_op jit(solution)/shard_map/all_to_all | solution.py:128
  (82 shorter events, 43.4 us)
Async XLA Ops:
  6.5 37.7 %copy-start = (f32[8]{0:T(128)S(1)}, f32[8]{0:T(128)}, u32[]{:S(2)}) copy-start(f32[8]{0:T(128)} %param.21) | copy-start | bytes 100
  6.5 37.2 %copy-start.3 = (f32[128]{0:T(128)S(1)}, f32[128]{0:T(128)}, u32[]{:S(2)}) copy-start(f32[128]{0:T(128)} %param.17) | copy-start | bytes 1540
  6.5 37.3 %copy-start.4 = (s32[128]{0:T(128)S(1)}, s32[128]{0:T(128)}, u32[]{:S(2)}) copy-start(s32[128]{0:T(128)} %param.18) | copy-start | bytes 1540
  6.5 37.3 %copy-start.5 = (f32[8]{0:T(128)S(1)}, f32[8]{0:T(128)}, u32[]{:S(2)}) copy-start(f32[8]{0:T(128)} %param.19) | copy-start | bytes 100
  6.5 37.5 %copy-start.6 = (f32[8]{0:T(128)S(1)}, f32[8]{0:T(128)}, u32[]{:S(2)}) copy-start(f32[8]{0:T(128)} %param.20) | copy-start | bytes 100
  8.0 12.1 %collective-permute-start = (f32[1,128,1,256]{3,2,0,1:T(1,128)S(1)}, f32[1,128,1,256]{3,2,0,1:T(1,128)S(1)}, u32[]{:S(2)}, u32[]{:S(2)}) collective-permute-start(f32[1,128,1,256]{3,2,0,1:T(1,128)S(1)} %get-tuple-element.272), channel_id=1, source_target_pairs={{1,0},{2,1},{3,2},{4,3},{5,4},{6,5},{7,6},{8,7},{9,8},{10,9},{11,1... | collective-permute-start | bytes 393224 | tf_op jit(solution)/shard_map/ppermute | solution.py:28
  16.8 3.9 %collective-permute-start.1 = (f32[1,128,1,256]{3,2,0,1:T(1,128)S(1)}, f32[1,128,1,256]{3,2,0,1:T(1,128)S(1)}, u32[]{:S(2)}, u32[]{:S(2)}) collective-permute-start(f32[1,128,1,256]{3,2,0,1:T(1,128)S(1)} %get-tuple-element.271), channel_id=1, source_target_pairs={{0,1},{1,2},{2,3},{3,4},{4,5},{5,6},{6,7},{7,8},{8,9},{9,10},{10,1... | collective-permute-start | bytes 393224 | tf_op jit(solution)/shard_map/ppermute | solution.py:26
  24.4 7.0 %collective-permute-start.2 = (f32[1,128,1,256]{3,2,0,1:T(1,128)S(1)}, f32[1,128,1,256]{3,2,0,1:T(1,128)S(1)}, u32[]{:S(2)}, u32[]{:S(2)}) collective-permute-start(f32[1,128,1,256]{3,2,0,1:T(1,128)S(1)} %get-tuple-element.270), channel_id=1, source_target_pairs={{1,0},{2,1},{3,2},{4,3},{5,4},{6,5},{7,6},{8,7},{9,8},{10,9},{11,1... | collective-permute-start | bytes 393224 | tf_op jit(solution)/shard_map/ppermute | solution.py:28
  26.3 6.3 %collective-permute-start.3 = (f32[1,128,1,256]{3,2,0,1:T(1,128)S(1)}, f32[1,128,1,256]{3,2,0,1:T(1,128)S(1)}, u32[]{:S(2)}, u32[]{:S(2)}) collective-permute-start(f32[1,128,1,256]{3,2,0,1:T(1,128)S(1)} %get-tuple-element.269), channel_id=1, source_target_pairs={{0,1},{1,2},{2,3},{3,4},{4,5},{5,6},{6,7},{7,8},{8,9},{9,10},{10,1... | collective-permute-start | bytes 393224 | tf_op jit(solution)/shard_map/ppermute | solution.py:26
  34.9 24.7 %all-to-all-start = ((f32[1,128,4,256]{3,2,0,1:T(4,128)}), f32[1,128,4,256]{3,2,0,1:T(4,128)S(1)}, u32[]{:S(2)}, u32[]{:S(2)}) async-start(f32[1,128,4,256]{3,2,0,1:T(4,128)} %add_multiply_fusion), calls=%async_computation | async-start | bytes 1048576 | tf_op jit(solution)/shard_map/all_to_all | solution.py:104
  43.6 102.3 %all-gather.9.cloned.1.call-start = ((), (), s32[]{:S(2)}) async-start(), calls=%async_computation.3 | async-start | bytes 4325376 | tf_op jit(solution)/shard_map/all_gather | solution.py:37
  62.5 171.5 %all-gather.11.cloned.1.call-start = ((), (), s32[]{:S(2)}) async-start(), calls=%async_computation.4 | async-start | bytes 4325376 | tf_op jit(solution)/shard_map/all_gather | solution.py:37
  63.2 258.7 %all-gather.7.cloned.1.call-start = ((), (), s32[]{:S(2)}) async-start(), calls=%async_computation.2 | async-start | bytes 4325376 | tf_op jit(solution)/shard_map/all_gather | solution.py:37
  233.9 40.5 %copy-start.2 = (f32[32,4,256]{2,1,0:T(4,128)S(1)}, f32[32,4,256]{2,1,0:T(4,128)}, u32[]{:S(2)}) copy-start(f32[32,4,256]{2,1,0:T(4,128)} %get-tuple-element.233) | copy-start | bytes 393220
  239.3 35.2 %copy-start.1 = (f32[32,4,256]{2,1,0:T(4,128)S(1)}, f32[32,4,256]{2,1,0:T(4,128)}, u32[]{:S(2)}) copy-start(f32[32,4,256]{2,1,0:T(4,128)} %get-tuple-element.235) | copy-start | bytes 393220
Sparse Core Ops, SparseCore 0:
  62.6 83.3 all-gather.8
  149.1 84.7 all-gather.10
  237.1 84.7 all-gather.6
where the time goes:
time: 388 us; the launch traced here: 382 us
  waiting for transfers between devices  231 us (60%)
  other arithmetic  78 us (20%)
  starting transfers between devices  25.8 us (7%)
  blocking collectives  18.3 us (5%)
  local copies, waits for them, and re-layouts  13.8 us (4%)
  between operations  13.3 us (3%)
    all_gather x3, waiting for transfers between devices, prefix(): pieces = jax.tree.map(lambda part: lax.all_gather(part, axis), value)  212 us
    select_n x62, other arithmetic, lap(): jnp.where(position < mine, new, old)  67.4 us
    all_to_all x1, blocking collectives, local(): lax.all_to_all(result, 'bins', split_axis=0, concat_axis=1, tiled=True)  18.3 us
    all_to_all x1, waiting for transfers between devices, local(): lax.all_to_all(level, 'bins', split_axis=1, concat_axis=0, tiled=True)  15.2 us
    ppermute x2, starting transfers between devices, extended(): lax.ppermute(head, axis, [((i + 1) % count, i) for i in range(ends)])  10.7 us
    rev x2, local copies, waits for them, and re-layouts, prefix(): pieces = jax.tree.map(lambda part: part[::-1], pieces)  10.7 us
    all_to_all x1, starting transfers between devices, local(): lax.all_to_all(level, 'bins', split_axis=1, concat_axis=0, tiled=True)  8.69 us
  transfers between devices with their start and end apart: 8, of which 7 were waited for; matrix products, arithmetic and copies ran while one was open for 12% of the time, Pallas kernels for 0%

commit v1 on v0

v1 whole, which is shorter than its diff:
```python
import jax
import jax.numpy as jnp
from jax import lax
from jax.sharding import PartitionSpec as P

NB = 128
NCLS = 8
HSUB = 2
VERTICAL_SUBSTEP = 2


h_diffusion = 0.2
v_diffusion = 0.2
step_duration = 0.5
collide_scale = 2.0


def extended(cells, sides, width):
    for axis, dim in sides:
        count = lax.axis_size(axis)
        ends = count - 1
        head = lax.slice_in_dim(cells, 0, width, axis=dim)
        tail = lax.slice_in_dim(cells, cells.shape[dim] - width, cells.shape[dim], axis=dim)
        cells = jnp.concatenate(
            [
                lax.ppermute(tail, axis, [(i, (i + 1) % count) for i in range(ends)]),
                cells,
                lax.ppermute(head, axis, [((i + 1) % count, i) for i in range(ends)]),
            ],
            axis=dim,
        )
    return cells


def settle_mix(column, sink):
    flux = sink * column
    above = jnp.concatenate([jnp.zeros_like(flux[:1]), flux[:-1]], 0)
    upper = jnp.concatenate([column[:1], column[:-1]], 0)
    lower = jnp.concatenate([column[1:], column[-1:]], 0)
    return column - flux + above + v_diffusion * (upper + lower - 2.0 * column)


def local(
    conc,
    vel_x,
    vel_y,
    sea_mask,
    settle,
    size_bin_kernel_class,
    aggregate_upward_factor,
    agg_down,
    break_rate,
):
    water = sea_mask.astype(jnp.float32)
    speed_x = vel_x[:, None]
    speed_y = vel_y[:, None]
    level = conc
    for unused_item in range(HSUB):
        padded = extended(level, (("xy", 2),), 1)
        east = padded[:, :, 2:, :]
        west = padded[:, :, :-2, :]
        side = jnp.pad(level, ((0, 0), (0, 0), (0, 0), (1, 1)))
        north = side[:, :, :, 2:]
        south = side[:, :, :, :-2]
        level = water * (
            level
            - 0.5 * speed_x * (east - west)
            - 0.5 * speed_y * (north - south)
            + h_diffusion * (east + west + north + south - 4.0 * level)
        )
    count_bins = lax.axis_size("bins")
    local_size_bins = NB // count_bins
    first_bin = lax.axis_index("bins") * local_size_bins
    sink = lax.dynamic_slice_in_dim(settle, first_bin, local_size_bins)[:, None, None]
    block = lax.all_to_all(level, "bins", split_axis=1, concat_axis=0, tiled=True)
    for unused_item in range(VERTICAL_SUBSTEP):
        block = settle_mix(block, sink)
    block = lax.all_to_all(block, "bins", split_axis=0, concat_axis=1, tiled=True)[0]
    onehot = (size_bin_kernel_class[:, None] == jnp.arange(NCLS)[None, :]).astype(jnp.float32)
    up, down, brk = (
        jnp.dot(onehot, table, precision=lax.Precision.HIGHEST)
        for table in (aggregate_upward_factor, agg_down, break_rate)
    )
    bins = jnp.arange(NB)
    weight = 1.0 / jnp.maximum(bins, 1).astype(jnp.float32)
    broken = (bins >= 1).astype(jnp.float32)
    lower = (bins[None, :] < bins[:, None]).astype(jnp.float32)
    higher = (bins[None, :] > bins[:, None]).astype(jnp.float32)
    scale = collide_scale / NB
    flat = block.reshape(NB, -1)
    sums = jnp.dot(
        jnp.concatenate([lower * up[None, :], higher * down[None, :], higher * (brk * weight)[None, :]], 0),
        flat,
        precision=lax.Precision.HIGHEST,
    ).reshape((3,) + block.shape)
    up, down, brk = (part[:, None, None] for part in (up, down, brk * broken))
    result = block + step_duration * (
        scale * (down * block * sums[0] - up * block * sums[1]) + sums[2] - brk * block
    )
    return result[None]


def solution(mesh):
    placed = (
        P("bins", None, "xy", None),
        P("bins", "xy", None),
        P("bins", "xy", None),
        P("xy", None),
        P(),
        P(),
        P(),
        P(),
        P(),
    )
    return jax.shard_map(
        local, mesh=mesh, in_specs=placed, out_specs=P("bins", None, "xy", None), check_vma=False
    )
```

time: 388 us -> 87.6 us (0.23)
  the two profiles are of different devices: /device:TPU:1 before, /device:TPU:26 now
where the time goes in v1:
time: 87.6 us; the launch traced here: 87 us
  waiting for transfers between devices  36.8 us (42%)
  starting transfers between devices  33.5 us (38%)
  other arithmetic  11 us (13%)
  local copies, waits for them, and re-layouts  3.27 us (4%)
  matrix products  2.09 us (2%)
    all_to_all x1, waiting for transfers between devices, local(): lax.all_to_all(block, 'bins', split_axis=0, concat_axis=1, tiled=True)[0]  17.2 us
    all_to_all x1, waiting for transfers between devices, local(): lax.all_to_all(level, 'bins', split_axis=1, concat_axis=0, tiled=True)  16.1 us
    all_to_all x1, starting transfers between devices, local(): lax.all_to_all(level, 'bins', split_axis=1, concat_axis=0, tiled=True)  13.5 us
    ppermute x2, starting transfers between devices, extended(): lax.ppermute(tail, axis, [(i, (i + 1) % count) for i in range(ends)])  8.07 us
    all_to_all x1, starting transfers between devices, local(): lax.all_to_all(block, 'bins', split_axis=0, concat_axis=1, tiled=True)[0]  6.45 us
    mul x2, other arithmetic, local(): water * (level - 0.5 * speed_x * (east - west) - 0.5 * speed_y * (north -...  6.22 us
    ppermute x2, starting transfers between devices, extended(): lax.ppermute(head, axis, [((i + 1) % count, i) for i in range(ends)])  5.56 us
    ppermute x2, waiting for transfers between devices, extended(): lax.ppermute(head, axis, [((i + 1) % count, i) for i in range(ends)])  3.59 us
  transfers between devices with their start and end apart: 6, of which 4 were waited for; matrix products, arithmetic and copies ran while one was open for 3% of the time, Pallas kernels for 0%

profile of v1, /device:TPU:26, one launch (start us, length us, event | category | flops | bytes accessed | tf_op | source)
XLA Modules:
  0.0 87.0 jit_solution(6476505913375497009)
XLA Ops:
  0.0 0.0 copy-start
  0.0 1.5 %fusion.35 = (f32[1,128,1,256]{3,2,0,1:T(1,128)S(1)}, f32[1,128,1,256]{3,2,0,1:T(1,128)S(1)}) fusion(f32[1,128,4,256]{3,2,0,1:T(4,128)} %bitcast.72), kind=kLoop, calls=%fused_computation.64 | loop fusion | bytes 524288 | tf_op jit(solution)/shard_map/slice | solution.py:23
  1.5 1.9 %collective-permute-start.1 = (f32[1,128,1,256]{3,2,0,1:T(1,128)S(1)}, f32[1,128,1,256]{3,2,0,1:T(1,128)S(1)}, u32[]{:S(2)}, u32[]{:S(2)}) collective-permute-start(f32[1,128,1,256]{3,2,0,1:T(1,128)S(1)} %get-tuple-element.20), channel_id=1, source_target_pairs={{0,1},{1,2},{2,3},{3,4},{4,5},{5,6},{6,7},{7,8},{8,9},{9,10},{10,1... | collective-permute-start | bytes 393224 | tf_op jit(solution)/shard_map/ppermute | solution.py:26
  3.4 3.6 %collective-permute-start = (f32[1,128,1,256]{3,2,0,1:T(1,128)S(1)}, f32[1,128,1,256]{3,2,0,1:T(1,128)S(1)}, u32[]{:S(2)}, u32[]{:S(2)}) collective-permute-start(f32[1,128,1,256]{3,2,0,1:T(1,128)S(1)} %get-tuple-element.21), channel_id=1, source_target_pairs={{1,0},{2,1},{3,2},{4,3},{5,4},{6,5},{7,6},{8,7},{9,8},{10,9},{11,1... | collective-permute-start | bytes 393224 | tf_op jit(solution)/shard_map/ppermute | solution.py:28
  7.1 0.7 convert_element_type.7
  7.8 0.7 multiply_bitcast_fusion
  8.5 0.0 collective-permute-done.1
  8.5 1.1 %collective-permute-done = f32[1,128,1,256]{3,2,0,1:T(1,128)S(1)} collective-permute-done((f32[1,128,1,256]{3,2,0,1:T(1,128)S(1)}, f32[1,128,1,256]{3,2,0,1:T(1,128)S(1)}, u32[]{:S(2)}, u32[]{:S(2)}) %collective-permute-start) | collective-permute-done | bytes 131104 | tf_op jit(solution)/shard_map/ppermute | solution.py:28
  9.6 3.9 %add_multiply_fusion.1 = f32[1,128,4,256]{3,2,0,1:T(4,128)S(1)} fusion(f32[1,128,4,256]{3,2,0,1:T(4,128)} %bitcast.73, f32[1,128,1,256]{3,2,0,1:T(1,128)S(1)} %collective-permute-done, f32[1,128,1,256]{3,2,0,1:T(1,128)S(1)} %collective-permute-done.1, f32[4,256]{1,0:T(4,128)S(1)} %get-tuple-element.24, f32[4,256]{1,0:T(4,128)S(1)} %get-tuple-element.25, ...), kind=kLoop, calls=%fused_computation.31 | loop fusion | flops 2097152 | bytes 1323008 | tf_op jit(solution)/shard_map/mul | solution.py:65
  13.5 0.0 copy-start.1
  13.5 0.2 fusion.34
  13.7 6.1 %collective-permute-start.3 = (f32[1,128,1,256]{3,2,0,1:T(1,128)S(1)}, f32[1,128,1,256]{3,2,0,1:T(1,128)S(1)}, u32[]{:S(2)}, u32[]{:S(2)}) collective-permute-start(f32[1,128,1,256]{3,2,0,1:T(1,128)S(1)} %get-tuple-element.18), channel_id=1, source_target_pairs={{0,1},{1,2},{2,3},{3,4},{4,5},{5,6},{6,7},{7,8},{8,9},{9,10},{10,1... | collective-permute-start | bytes 393224 | tf_op jit(solution)/shard_map/ppermute | solution.py:26
  19.9 1.9 %collective-permute-start.2 = (f32[1,128,1,256]{3,2,0,1:T(1,128)S(1)}, f32[1,128,1,256]{3,2,0,1:T(1,128)S(1)}, u32[]{:S(2)}, u32[]{:S(2)}) collective-permute-start(f32[1,128,1,256]{3,2,0,1:T(1,128)S(1)} %get-tuple-element.19), channel_id=1, source_target_pairs={{1,0},{2,1},{3,2},{4,3},{5,4},{6,5},{7,6},{8,7},{9,8},{10,9},{11,1... | collective-permute-start | bytes 393224 | tf_op jit(solution)/shard_map/ppermute | solution.py:28
  21.8 0.0 collective-permute-done.3
  21.8 2.5 %collective-permute-done.2 = f32[1,128,1,256]{3,2,0,1:T(1,128)S(1)} collective-permute-done((f32[1,128,1,256]{3,2,0,1:T(1,128)S(1)}, f32[1,128,1,256]{3,2,0,1:T(1,128)S(1)}, u32[]{:S(2)}, u32[]{:S(2)}) %collective-permute-start.2) | collective-permute-done | bytes 131104 | tf_op jit(solution)/shard_map/ppermute | solution.py:28
  24.3 2.3 %add_multiply_fusion = f32[1,128,4,256]{3,2,0,1:T(4,128)} fusion(f32[1,128,4,256]{3,2,0,1:T(4,128)S(1)} %add_multiply_fusion.1, f32[1,128,1,256]{3,2,0,1:T(1,128)S(1)} %collective-permute-done.2, f32[1,128,1,256]{3,2,0,1:T(1,128)S(1)} %collective-permute-done.3, f32[4,256]{1,0:T(4,128)S(1)} %get-tuple-element.24, f32[4,256]{1,0:T(4,128)S(1)} %get-tuple-element.25, ...), kind=kLoop, calls=%fused_computation.30 | loop fusion | flops 2097152 | bytes 1323008 | tf_op jit(solution)/shard_map/mul | solution.py:65
  26.6 13.5 %all-to-all-start = ((f32[1,128,4,256]{3,2,0,1:T(4,128)}), f32[1,128,4,256]{3,2,0,1:T(4,128)S(1)}, u32[]{:S(2)}, u32[]{:S(2)}) async-start(f32[1,128,4,256]{3,2,0,1:T(4,128)} %add_multiply_fusion), calls=%async_computation | async-start | bytes 1048576 | tf_op jit(solution)/shard_map/all_to_all | solution.py:75
  40.1 0.0 copy-done.1
  40.1 0.1 dynamic_slice.3
  40.2 16.1 %all-to-all-done = f32[1,128,4,256]{3,2,0,1:T(4,128)S(1)} async-done(((f32[1,128,4,256]{3,2,0,1:T(4,128)}), f32[1,128,4,256]{3,2,0,1:T(4,128)S(1)}, u32[]{:S(2)}, u32[]{:S(2)}) %all-to-all-start) | async-done | bytes 524320 | tf_op jit(solution)/shard_map/all_to_all | solution.py:75
  56.2 0.2 broadcast_multiply_fusion.1
  56.5 0.1 fusion.33
  56.6 0.6 broadcast_multiply_fusion
  57.2 0.2 fusion.31
  57.5 0.0 copy-start.2
  57.5 0.0 copy-start.4
  57.5 0.0 copy-start.3
  57.5 1.3 %fusion.5 = f32[32,4,4,256]{3,2,1,0:T(4,128)} fusion(f32[31,4,4,256]{3,2,1,0:T(4,128)S(1)} %get-tuple-element.11, f32[1,4,4,256]{3,2,1,0:T(4,128)S(1)} %get-tuple-element.13, f32[1,4,4,256]{3,2,1,0:T(4,128)S(1)} %get-tuple-element.12, f32[31,4,4,256]{3,2,1,0:T(4,128)S(1)} %get-tuple-element.10, f32[32,4,4,256]{3,2,1,0:T(4,128)S(1)} %get-tuple-element.6, ...), kind=kLoop, calls=%fused_computation.18 | loop fusion | flops 1310720 | bytes 2605072 | tf_op jit(solution)/shard_map/add | solution.py:40
  58.8 6.5 %all-to-all-start.1 = ((f32[32,4,4,256]{3,2,1,0:T(4,128)}), f32[32,4,4,256]{3,2,1,0:T(4,128)S(1)}, u32[]{:S(2)}, u32[]{:S(2)}) async-start(f32[32,4,4,256]{3,2,1,0:T(4,128)} %fusion.5), calls=%async_computation.1 | async-start | bytes 1048576 | tf_op jit(solution)/shard_map/all_to_all | solution.py:78
  65.3 0.0 copy-done.2
  65.3 0.0 copy-done.4
  65.3 0.2 convolution_bitcast_fusion.1
  65.5 0.0 copy-done.3
  65.5 0.3 convolution_bitcast_fusion.2
  65.8 0.0 copy-done
  65.8 0.3 compare_select_fusion
  66.0 0.1 fusion.21
  66.1 17.2 %all-to-all-done.1 = f32[32,4,4,256]{3,2,1,0:T(4,128)S(1)} async-done(((f32[32,4,4,256]{3,2,1,0:T(4,128)}), f32[32,4,4,256]{3,2,1,0:T(4,128)S(1)}, u32[]{:S(2)}, u32[]{:S(2)}) %all-to-all-start.1) | async-done | bytes 524320 | tf_op jit(solution)/shard_map/all_to_all | solution.py:78
  83.3 0.1 copy.19
  83.4 1.4 %fusion.13 = f32[384,1024]{1,0:T(8,128)S(1)} fusion(f32[128,1024]{1,0:T(8,128)S(1)} %bitcast.69, f32[128,128]{1,0:T(8,128)S(1)} %get-tuple-element.26, f32[128,128]{1,0:T(8,128)S(1)} %get-tuple-element.27, f32[128,128]{1,0:T(8,128)S(1)} %fusion.21), kind=kOutput, calls=%fused_computation.34 | convolution fusion | flops 604078080 | bytes 2293760 | tf_op jit(solution)/shard_map/dot_general | solution.py:91
  84.8 0.2 fusion.30
  85.0 0.3 squeeze.14
  85.2 0.2 squeeze.15
  85.5 0.2 squeeze.13
  85.7 1.3 %bitcast_add_fusion = f32[1,128,4,256]{3,2,1,0:T(4,128)} fusion(f32[1,128,4,256]{3,2,1,0:T(4,128)S(1)} %squeeze.15, f32[1,128,4,256]{3,2,1,0:T(4,128)S(1)} %squeeze.13, f32[1,128,4,256]{3,2,1,0:T(4,128)S(1)} %squeeze.14, f32[128]{0:T(128)S(1)} %get-tuple-element.22, f32[128]{0:T(128)S(1)} %convolution_bitcast_fusion.1, f32[128]{0:T(128)S(1)} %convolution_bitcast_fusion.2, ...), kind=kLoop, calls=%fused_computation.19 | loop fusion | flops 1441792 | bytes 2622976 | tf_op jit(solution)/shard_map/add | solution.py:97
  (5 shorter events, 0.1 us)
Async XLA Ops:
  0.0 65.8 %copy-start = (f32[8]{0:T(128)S(1)}, f32[8]{0:T(128)}, u32[]{:S(2)}) copy-start(f32[8]{0:T(128)} %param.17) | copy-start | bytes 100
  1.5 7.0 %collective-permute-start.1 = (f32[1,128,1,256]{3,2,0,1:T(1,128)S(1)}, f32[1,128,1,256]{3,2,0,1:T(1,128)S(1)}, u32[]{:S(2)}, u32[]{:S(2)}) collective-permute-start(f32[1,128,1,256]{3,2,0,1:T(1,128)S(1)} %get-tuple-element.20), channel_id=1, source_target_pairs={{0,1},{1,2},{2,3},{3,4},{4,5},{5,6},{6,7},{7,8},{8,9},{9,10},{10,1... | collective-permute-start | bytes 393224 | tf_op jit(solution)/shard_map/ppermute | solution.py:26
  3.4 6.1 %collective-permute-start = (f32[1,128,1,256]{3,2,0,1:T(1,128)S(1)}, f32[1,128,1,256]{3,2,0,1:T(1,128)S(1)}, u32[]{:S(2)}, u32[]{:S(2)}) collective-permute-start(f32[1,128,1,256]{3,2,0,1:T(1,128)S(1)} %get-tuple-element.21), channel_id=1, source_target_pairs={{1,0},{2,1},{3,2},{4,3},{5,4},{6,5},{7,6},{8,7},{9,8},{10,9},{11,1... | collective-permute-start | bytes 393224 | tf_op jit(solution)/shard_map/ppermute | solution.py:28
  13.5 26.6 %copy-start.1 = (f32[128]{0:T(128)S(1)}, f32[128]{0:T(128)}, u32[]{:S(2)}) copy-start(f32[128]{0:T(128)} %param.13) | copy-start | bytes 1540
  13.7 8.1 %collective-permute-start.3 = (f32[1,128,1,256]{3,2,0,1:T(1,128)S(1)}, f32[1,128,1,256]{3,2,0,1:T(1,128)S(1)}, u32[]{:S(2)}, u32[]{:S(2)}) collective-permute-start(f32[1,128,1,256]{3,2,0,1:T(1,128)S(1)} %get-tuple-element.18), channel_id=1, source_target_pairs={{0,1},{1,2},{2,3},{3,4},{4,5},{5,6},{6,7},{7,8},{8,9},{9,10},{10,1... | collective-permute-start | bytes 393224 | tf_op jit(solution)/shard_map/ppermute | solution.py:26
  19.9 4.4 %collective-permute-start.2 = (f32[1,128,1,256]{3,2,0,1:T(1,128)S(1)}, f32[1,128,1,256]{3,2,0,1:T(1,128)S(1)}, u32[]{:S(2)}, u32[]{:S(2)}) collective-permute-start(f32[1,128,1,256]{3,2,0,1:T(1,128)S(1)} %get-tuple-element.19), channel_id=1, source_target_pairs={{1,0},{2,1},{3,2},{4,3},{5,4},{6,5},{7,6},{8,7},{9,8},{10,9},{11,1... | collective-permute-start | bytes 393224 | tf_op jit(solution)/shard_map/ppermute | solution.py:28
  26.6 29.6 %all-to-all-start = ((f32[1,128,4,256]{3,2,0,1:T(4,128)}), f32[1,128,4,256]{3,2,0,1:T(4,128)S(1)}, u32[]{:S(2)}, u32[]{:S(2)}) async-start(f32[1,128,4,256]{3,2,0,1:T(4,128)} %add_multiply_fusion), calls=%async_computation | async-start | bytes 1048576 | tf_op jit(solution)/shard_map/all_to_all | solution.py:75
  57.5 7.8 %copy-start.2 = (f32[8]{0:T(128)S(1)}, f32[8]{0:T(128)}, u32[]{:S(2)}) copy-start(f32[8]{0:T(128)} %param.15) | copy-start | bytes 100
  57.5 7.8 %copy-start.4 = (s32[128]{0:T(128)S(1)}, s32[128]{0:T(128)}, u32[]{:S(2)}) copy-start(s32[128]{0:T(128)} %param.14) | copy-start | bytes 1540
  57.5 8.0 %copy-start.3 = (f32[8]{0:T(128)S(1)}, f32[8]{0:T(128)}, u32[]{:S(2)}) copy-start(f32[8]{0:T(128)} %param.16) | copy-start | bytes 100
  58.8 24.5 %all-to-all-start.1 = ((f32[32,4,4,256]{3,2,1,0:T(4,128)}), f32[32,4,4,256]{3,2,1,0:T(4,128)S(1)}, u32[]{:S(2)}, u32[]{:S(2)}) async-start(f32[32,4,4,256]{3,2,1,0:T(4,128)} %fusion.5), calls=%async_computation.1 | async-start | bytes 1048576 | tf_op jit(solution)/shard_map/all_to_all | solution.py:78

commit v2 on v1

v2 whole, which is shorter than its diff:
```python
import functools

import jax
import jax.numpy as jnp
from jax import lax
from jax.experimental import pallas as pl
from jax.experimental.pallas import tpu as pltpu
from jax.sharding import PartitionSpec as P

NB = 128
NCLS = 8

h_diffusion = 0.2
v_diffusion = 0.2
step_duration = 0.5
collide_scale = 2.0

MESH = pl.DeviceIdType.MESH
SUB, LANE = 8, 128
RING = 4
GROUP = NB // RING
PIECES = 4
PART = GROUP // PIECES
PAIRS = PART // 2
OFFSETS = (2, 1, 3, 0)
AUX = 2
MESSAGE = AUX + RING * PAIRS


def turn(value, shift, axis):
    return pltpu.roll(value, shift % value.shape[axis], axis)


def step_kernel(
    depth,
    bands,
    conc,
    vel_x,
    vel_y,
    sea_mask,
    settle,
    classes,
    up_table,
    down_table,
    break_table,
    out,
    up_out,
    down_out,
    up_in,
    down_in,
    moved,
    column,
    mixed,
    settled,
    rates,
    up_send,
    up_recv,
    down_send,
    down_recv,
    ring_send,
    ring_recv,
    deep_send,
    deep_recv,
    back_send,
    back_recv,
):
    place = lax.axis_index("bins")
    band = lax.axis_index("xy")
    z, x = place // RING, place % RING
    before, after = (band + bands - 1) % bands, (band + 1) % bands
    above, below = (z + depth - 1) % depth, (z + 1) % depth
    peers = [(place, before), (place, after), (above * RING + x, band), (below * RING + x, band)]
    peers += [(z * RING + (x + d) % RING, band) for d in (1, 2, 3)]
    barrier = pltpu.get_barrier_semaphore()
    for peer in peers:
        pl.semaphore_signal(barrier, inc=1, device_id=peer, device_id_type=MESH)

    sub = lax.broadcasted_iota(jnp.int32, (SUB, LANE), 0)
    lane = lax.broadcasted_iota(jnp.int32, (SUB, LANE), 1)
    row = sub % 4
    low = row < 2
    row_first, row_last = row == 0, row == 3
    lane_first, lane_last = lane == 0, lane == LANE - 1
    half = sub < 4
    main_seam = (half & lane_first) | (~half & lane_last)
    side_seam = (~half & lane_first) | (half & lane_last)
    keep_up = (band > 0).astype(jnp.float32)
    keep_down = (band < bands - 1).astype(jnp.float32)

    def pack(first, second):
        return (
            jnp.where(low, turn(first, 4, 0), turn(second, 6, 0)) * keep_up,
            jnp.where(low, turn(first, 2, 0), turn(second, 4, 0)) * keep_down,
        )

    def unpack(upper, lower):
        return (
            jnp.where(low, upper, turn(lower, 2, 0)),
            jnp.where(low, turn(upper, 6, 0), lower),
        )

    def plane(ref):
        whole = ref[...].reshape(4, 2 * LANE)
        return jnp.concatenate([whole[:, :LANE], whole[:, LANE:]], 0)

    water = plane(sea_mask).astype(jnp.float32)
    speed_x, speed_y = plane(vel_x), plane(vel_y)
    for spot, pair in enumerate(((speed_x, speed_y), (water, water))):
        upper, lower = pack(*pair)
        up_out[0, spot] = upper
        down_out[0, spot] = lower

    def fill(j, unused):
        for n, d in enumerate(OFFSETS):
            first = (x + d) % RING * GROUP + j * PART
            for t in range(PAIRS):
                upper, lower = pack(conc[first + 2 * t], conc[first + 2 * t + 1])
                up_out[j, AUX + n * PAIRS + t] = upper
                down_out[j, AUX + n * PAIRS + t] = lower
        return unused

    lax.fori_loop(0, PIECES, fill, 0)
    pl.semaphore_wait(barrier, len(peers))

    def halo(j, start):
        rows = pl.ds(start, MESSAGE - start)
        return (
            pltpu.make_async_remote_copy(
                src_ref=up_out.at[j, rows],
                dst_ref=up_in.at[j, rows],
                send_sem=up_send.at[j],
                recv_sem=up_recv.at[j],
                device_id=(place, before),
                device_id_type=MESH,
            ),
            pltpu.make_async_remote_copy(
                src_ref=down_out.at[j, rows],
                dst_ref=down_in.at[j, rows],
                send_sem=down_send.at[j],
                recv_sem=down_recv.at[j],
                device_id=(place, after),
                device_id_type=MESH,
            ),
        )

    def ring(j, d):
        return pltpu.make_async_remote_copy(
            src_ref=moved.at[d, pl.ds(j * PART, PART)],
            dst_ref=column.at[2 + x, pl.ds(j * PART, PART)],
            send_sem=ring_send.at[j, d],
            recv_sem=ring_recv.at[j, d],
            device_id=(z * RING + (x + d) % RING, band),
            device_id_type=MESH,
        )

    def deep(j):
        part = pl.ds(j * PART, PART)
        return (
            pltpu.make_async_remote_copy(
                src_ref=column.at[pl.ds(4, 2), part],
                dst_ref=column.at[pl.ds(0, 2), part],
                send_sem=deep_send.at[j, 0],
                recv_sem=deep_recv.at[j, 0],
                device_id=(below * RING + x, band),
                device_id_type=MESH,
            ),
            pltpu.make_async_remote_copy(
                src_ref=column.at[pl.ds(2, 2), part],
                dst_ref=column.at[pl.ds(6, 2), part],
                send_sem=deep_send.at[j, 1],
                recv_sem=deep_recv.at[j, 1],
                device_id=(above * RING + x, band),
                device_id_type=MESH,
            ),
        )

    def back(j, d):
        part = pl.ds(j * PART, PART)
        return pltpu.make_async_remote_copy(
            src_ref=mixed.at[(x + d) % RING, part],
            dst_ref=settled.at[x, part],
            send_sem=back_send.at[j, d],
            recv_sem=back_recv.at[j, d],
            device_id=(z * RING + (x + d) % RING, band),
            device_id_type=MESH,
        )

    for j in range(PIECES):
        for copy in halo(j, 0 if j == 0 else AUX):
            copy.start()

    def rate(b, unused):
        own = classes[b]
        bin_index = jnp.maximum(b, 1).astype(jnp.float32)
        r = step_duration * break_table[own]
        rates[0, b] = up_table[own]
        rates[1, b] = down_table[own]
        rates[2, b] = r / bin_index
        rates[3, b] = 1.0 - r * jnp.minimum(b, 1).astype(jnp.float32)
        return unused

    lax.fori_loop(0, NB, rate, 0)

    def weights(mask, along, across):
        return (
            (1.0 - 4.0 * h_diffusion) * mask,
            mask * (h_diffusion - 0.5 * along),
            mask * (h_diffusion + 0.5 * along),
            mask * (h_diffusion - 0.5 * across),
            mask * (h_diffusion + 0.5 * across),
        )

    def transport(cells, rest, seam, factors):
        own, east_f, west_f, north_f, south_f = factors
        east = turn(jnp.where(row_first, rest, cells), -1, 0)
        west = turn(jnp.where(row_last, rest, cells), 1, 0)
        swapped = jnp.where(seam, turn(cells, 4, 0), 0.0)
        north = turn(jnp.where(lane_first, swapped, cells), -1, 1)
        south = turn(jnp.where(lane_last, swapped, cells), 1, 1)
        return own * cells + east_f * east + west_f * west + north_f * north + south_f * south

    main = weights(water, speed_x, speed_y)
    for copy in halo(0, 0):
        copy.wait_recv()
    side_x, side_y = unpack(up_in[0, 0], down_in[0, 0])
    side_water, _ = unpack(up_in[0, 1], down_in[0, 1])
    side = weights(side_water, side_x, side_y)

    def horizontal(j, unused):
        @pl.when(j > 0)
        def _():
            for copy in halo(j, AUX):
                copy.wait_recv()

        for n, d in enumerate(OFFSETS):
            first = (x + d) % RING * GROUP + j * PART
            for t in range(PAIRS):
                spot = AUX + n * PAIRS + t
                rests = unpack(up_in[j, spot], down_in[j, spot])
                for i, rest in enumerate(rests):
                    cells = conc[first + 2 * t + i]
                    once = transport(cells, rest, main_seam, main)
                    rest = transport(rest, cells, side_seam, side)
                    twice = transport(once, rest, main_seam, main)
                    if d:
                        moved[d, j * PART + 2 * t + i] = twice
                    else:
                        column[2 + x, j * PART + 2 * t + i] = twice
            if d:
                ring(j, d).start()
        return unused

    lax.fori_loop(0, PIECES, horizontal, 0)

    def forward(j):
        for d in (1, 2, 3):
            ring(j, d).wait_recv()
        for copy in deep(j):
            copy.start()

    top, bottom = z == 0, z == depth - 1

    def settle_mix(levels, sink, start):
        share = v_diffusion
        keep, fall = 1.0 - 2.0 * share - sink, share + sink
        count = len(levels) - 2
        fresh = []
        for k in range(count):
            upper, own, lower = levels[k : k + 3]
            upper_term = fall * upper
            lower_term = share * lower
            if start + k == 2:
                upper_term = jnp.where(top, share * own, upper_term)
            if start + k == 5:
                lower_term = jnp.where(bottom, share * own, lower_term)
            fresh.append(keep * own + upper_term + lower_term)
        return fresh

    def vertical(j):
        for copy in deep(j):
            copy.wait_recv()
        for i in range(PART):
            spot = j * PART + i
            sink = settle[x * GROUP + spot]
            levels = [column[k, spot] for k in range(8)]
            levels = settle_mix(settle_mix(levels, sink, 1), sink, 2)
            for k in range(RING):
                mixed[k, spot] = levels[k]
            settled[x, spot] = mixed[x, spot]
        for d in (2, 1, 3):
            back(j, d).start()

    forward(0)

    def middle(j, unused):
        forward(j)
        vertical(j - 1)
        return unused

    lax.fori_loop(1, PIECES, middle, 0)
    vertical(PIECES - 1)

    def arrive(j, unused):
        for d in (1, 2, 3):
            back(j, d).wait_recv()
        return unused

    lax.fori_loop(0, PIECES, arrive, 0)

    zero = jnp.zeros((SUB, LANE), jnp.float32)

    def totals(b, sums):
        higher, pieces = sums
        cells = settled[b // GROUP, b % GROUP]
        return higher + rates[1, b] * cells, pieces + rates[2, b] * cells

    higher, pieces = lax.fori_loop(0, NB, totals, (zero, zero), unroll=8)

    def collide(b, sums):
        lower, higher, pieces = sums
        cells = settled[b // GROUP, b % GROUP]
        gain, loss = rates[1, b], rates[0, b]
        higher = higher - gain * cells
        pieces = pieces - rates[2, b] * cells
        change = (step_duration * collide_scale / NB) * (gain * lower - loss * higher)
        out[b] = cells * (rates[3, b] + change) + pieces
        return lower + loss * cells, higher, pieces

    lax.fori_loop(0, NB, collide, (zero, higher, pieces), unroll=8)

    for j in range(PIECES):
        for copy in halo(j, 0 if j == 0 else AUX):
            copy.wait_send()

    def drain(j, unused):
        for d in (1, 2, 3):
            ring(j, d).wait_send()
            back(j, d).wait_send()
        for copy in deep(j):
            copy.wait_send()
        return unused

    lax.fori_loop(0, PIECES, drain, 0)


def local(depth, bands, conc, *rest):
    cells = conc.reshape(NB, 4, 2, LANE).transpose(0, 2, 1, 3).reshape(NB, SUB, LANE)
    vmem = pl.BlockSpec(memory_space=pltpu.VMEM)
    smem = pl.BlockSpec(memory_space=pltpu.SMEM)
    dma = pltpu.SemaphoreType.DMA
    tile = (SUB, LANE)

    def buffer(*shape):
        return pltpu.VMEM(shape + tile, jnp.float32)

    result = pl.pallas_call(
        functools.partial(step_kernel, depth, bands),
        out_shape=jax.ShapeDtypeStruct((NB,) + tile, jnp.float32),
        in_specs=[vmem] * 4 + [smem] * 5,
        out_specs=vmem,
        scratch_shapes=[
            buffer(PIECES, MESSAGE),
            buffer(PIECES, MESSAGE),
            buffer(PIECES, MESSAGE),
            buffer(PIECES, MESSAGE),
            buffer(RING, GROUP),
            buffer(8, GROUP),
            buffer(RING, GROUP),
            buffer(RING, GROUP),
            pltpu.SMEM((4, NB), jnp.float32),
            dma((PIECES,)),
            dma((PIECES,)),
            dma((PIECES,)),
            dma((PIECES,)),
            dma((PIECES, RING)),
            dma((PIECES, RING)),
            dma((PIECES, 2)),
            dma((PIECES, 2)),
            dma((PIECES, RING)),
            dma((PIECES, RING)),
        ],
        compiler_params=pltpu.CompilerParams(collective_id=0, has_side_effects=True),
    )(cells, *rest)
    return result.reshape(NB, 2, 4, LANE).transpose(0, 2, 1, 3).reshape(conc.shape)


def solution(mesh):
    placed = (
        P("bins", None, "xy", None),
        P("bins", "xy", None),
        P("bins", "xy", None),
        P("xy", None),
        P(),
        P(),
        P(),
        P(),
        P(),
    )
    return jax.shard_map(
        functools.partial(local, mesh.shape["bins"] // RING, mesh.shape["xy"]),
        mesh=mesh,
        in_specs=placed,
        out_specs=P("bins", None, "xy", None),
        check_vma=False,
    )
```

time: 87.6 us -> 42 us (0.48)
  the two profiles are of different devices: /device:TPU:26 before, /device:TPU:56 now
where the time goes in v2:
time: 42 us; the launch traced here: 41.8 us
  Pallas kernels  39.9 us (95%)
  local copies, waits for them, and re-layouts  1.87 us (4%)
    pallas_call x1, Pallas kernels, local(): pl.pallas_call(functools.partial(step_kernel, depth, bands), out_shape=ja...  39.9 us
    unnamed x1, local copies, waits for them, and re-layouts  1.87 us

profile of v2, /device:TPU:56, one launch (start us, length us, event | category | flops | bytes accessed | tf_op | source)
XLA Modules:
  0.0 41.8 jit_solution(7121125729534121290)
XLA Ops:
  0.0 39.9 %shard_map.91 = f32[128,8,128]{2,1,0:T(8,128)} custom-call(f32[128,8,128]{2,1,0:T(8,128)} %bitcast.11, f32[1,4,256]{2,1,0:T(4,128)} %vel_x.1, f32[1,4,256]{2,1,0:T(4,128)} %vel_y.1, s32[4,256]{1,0:T(4,128)} %sea_mask.1, f32[128]{0:T(128)} %settle.1, s32[128]{0:T(128)} %classes.1, f32[8]{0:T(128)} %up_table.1, f32[8]{0:T(128)} %down_table.1, f32[8]{0:T(128)} %break_table.1), custom_call_target="tpu_custom_call" | custom-call | tf_op jit(solution)/shard_map/pallas_call | solution.py:356
  39.9 1.9 %copy.13 = f32[1,128,4,256]{3,2,1,0:T(4,128)} copy(f32[1,128,4,256]{3,2,1,0:T(4,128)} %bitcast.10) | data formatting | bytes 1048576

commit v3 on v2

v3 whole, which is shorter than its diff:
```python
import functools

import jax
import jax.numpy as jnp
from jax import lax
from jax.experimental import pallas as pl
from jax.experimental.pallas import tpu as pltpu
from jax.sharding import PartitionSpec as P

NB = 128
NCLS = 8

h_diffusion = 0.2
v_diffusion = 0.2
step_duration = 0.5
collide_scale = 2.0

MESH = pl.DeviceIdType.MESH
SUB, LANE = 8, 128
RING = 4
GROUP = NB // RING
PIECES = 4
PART = GROUP // PIECES
QUADS = PART // 4
OFFSETS = (2, 1, 3, 0)
AUX = 3
MESSAGE = AUX + RING * QUADS * 2
ALPHA = step_duration * collide_scale / NB


def turn(value, shift, axis):
    return pltpu.roll(value, shift % value.shape[axis], axis)


def step_kernel(
    depth,
    bands,
    conc_hbm,
    vel_x_hbm,
    vel_y_hbm,
    sea_mask_hbm,
    settle_hbm,
    classes_hbm,
    up_hbm,
    down_hbm,
    break_hbm,
    settled,
    tables,
    conc,
    vel_x,
    vel_y,
    sea_mask,
    settle,
    classes,
    up_table,
    down_table,
    break_table,
    up_out,
    down_out,
    up_in,
    down_in,
    moved,
    column,
    mixed,
    sinks,
    factors,
    load_sem,
    enter_sem,
    up_send,
    up_recv,
    down_send,
    down_recv,
    ring_send,
    ring_recv,
    deep_send,
    deep_recv,
    back_send,
    back_recv,
):
    place = lax.axis_index("bins")
    band = lax.axis_index("xy")
    z, x = place // RING, place % RING
    top, bottom = z == 0, z == depth - 1
    first_band, last_band = band == 0, band == bands - 1
    barrier = pltpu.get_barrier_semaphore()

    def greet(bins, xy):
        pl.semaphore_signal(barrier, inc=1, device_id=(bins, xy), device_id_type=MESH)

    for d in (1, 2, 3):
        greet(z * RING + (x + d) % RING, band)
    pl.when(~first_band)(lambda: greet(place, band - 1))
    pl.when(~last_band)(lambda: greet(place, band + 1))
    pl.when(~bottom)(lambda: greet(place + RING, band))

    loads = [
        pltpu.make_async_copy(src, dst, load_sem.at[i])
        for i, (src, dst) in enumerate(
            (
                (conc_hbm, conc),
                (vel_x_hbm, vel_x),
                (vel_y_hbm, vel_y),
                (sea_mask_hbm, sea_mask),
                (settle_hbm, settle),
                (classes_hbm, classes),
                (up_hbm, up_table),
                (down_hbm, down_table),
                (break_hbm, break_table),
            )
        )
    ]
    for copy in loads:
        copy.start()

    zero = jnp.zeros((SUB, LANE), jnp.float32)

    @pl.when(first_band)
    def _():
        down_in[...] = jnp.zeros_like(down_in)

    @pl.when(last_band)
    def _():
        up_in[...] = jnp.zeros_like(up_in)

    sub = lax.broadcasted_iota(jnp.int32, (SUB, LANE), 0)
    lane = lax.broadcasted_iota(jnp.int32, (SUB, LANE), 1)
    even = sub % 2 == 0
    low = sub % 4 < 2
    lane_first, lane_last = lane == 0, lane == LANE - 1
    half = sub < 4
    seam = (half & lane_first) | (~half & lane_last)

    def swap_rows(a, b, c, d):
        ab, ba = jnp.where(even, a, turn(b, 1, 0)), jnp.where(even, turn(a, -1, 0), b)
        cd, dc = jnp.where(even, c, turn(d, 1, 0)), jnp.where(even, turn(c, -1, 0), d)
        return (
            jnp.where(low, ab, turn(cd, 2, 0)),
            jnp.where(low, ba, turn(dc, 2, 0)),
            jnp.where(low, turn(ab, -2, 0), cd),
            jnp.where(low, turn(ba, -2, 0), dc),
        )

    for copy in loads:
        copy.wait()

    def plane(ref):
        whole = ref[...].reshape(4, 2 * LANE)
        return jnp.concatenate([whole[:, :LANE], whole[:, LANE:]], 0)

    fields = [
        swap_rows(*[value] * 4)
        for value in (plane(vel_x), plane(vel_y), plane(sea_mask).astype(jnp.float32))
    ]
    for k, rows in enumerate(fields):
        up_out[0, k] = rows[0]
        down_out[0, k] = rows[3]

    def pack(j):
        for n, d in enumerate(OFFSETS):
            for q in range(QUADS):
                first = (x + d) % RING * GROUP + j * PART + 4 * q
                rows = swap_rows(*[conc[first + i] for i in range(4)])
                spot = AUX + (n * QUADS + q) * 2
                up_out[j, spot], up_out[j, spot + 1] = rows[0], rows[1]
                down_out[j, spot], down_out[j, spot + 1] = rows[2], rows[3]

    def halo_up(j, start):
        rows = pl.ds(start, MESSAGE - start)
        return pltpu.make_async_remote_copy(
            src_ref=up_out.at[j, rows],
            dst_ref=up_in.at[j, rows],
            send_sem=up_send.at[j],
            recv_sem=up_recv.at[j],
            device_id=(place, band - 1),
            device_id_type=MESH,
        )

    def halo_down(j, start):
        rows = pl.ds(start, MESSAGE - start)
        return pltpu.make_async_remote_copy(
            src_ref=down_out.at[j, rows],
            dst_ref=down_in.at[j, rows],
            send_sem=down_send.at[j],
            recv_sem=down_recv.at[j],
            device_id=(place, band + 1),
            device_id_type=MESH,
        )

    def ring(j, d):
        return pltpu.make_async_remote_copy(
            src_ref=moved.at[d, pl.ds(j * PART, PART)],
            dst_ref=column.at[2 + x, pl.ds(j * PART, PART)],
            send_sem=ring_send.at[j, d],
            recv_sem=ring_recv.at[j, d],
            device_id=(z * RING + (x + d) % RING, band),
            device_id_type=MESH,
        )

    def deep_down(j):
        part = pl.ds(j * PART, PART)
        return pltpu.make_async_remote_copy(
            src_ref=column.at[pl.ds(4, 2), part],
            dst_ref=column.at[pl.ds(0, 2), part],
            send_sem=deep_send.at[j, 0],
            recv_sem=deep_recv.at[j, 0],
            device_id=(place + RING, band),
            device_id_type=MESH,
        )

    def deep_up(j):
        part = pl.ds(j * PART, PART)
        return pltpu.make_async_remote_copy(
            src_ref=column.at[pl.ds(2, 2), part],
            dst_ref=column.at[pl.ds(6, 2), part],
            send_sem=deep_send.at[j, 1],
            recv_sem=deep_recv.at[j, 1],
            device_id=(place - RING, band),
            device_id_type=MESH,
        )

    def back(j, d):
        part = pl.ds(j * PART, PART)
        return pltpu.make_async_remote_copy(
            src_ref=mixed.at[(x + d) % RING, part],
            dst_ref=settled.at[x, part],
            send_sem=back_send.at[j, d],
            recv_sem=back_recv.at[j, d],
            device_id=(z * RING + (x + d) % RING, band),
            device_id_type=MESH,
        )

    def send_halo(j, start):
        pl.when(~first_band)(lambda: halo_up(j, start).start())
        pl.when(~last_band)(lambda: halo_down(j, start).start())

    def take_halo(j, start):
        pl.when(~last_band)(lambda: halo_up(j, start).wait_recv())
        pl.when(~first_band)(lambda: halo_down(j, start).wait_recv())

    pack(0)
    greeted = 3 + (1 - first_band.astype(jnp.int32)) + (1 - last_band.astype(jnp.int32))
    pl.semaphore_wait(barrier, greeted + (1 - top.astype(jnp.int32)))
    send_halo(0, 0)

    @pl.when(~top)
    def _():
        pl.semaphore_signal(
            enter_sem, inc=1, device_id=(place - RING, band), device_id_type=MESH
        )

    def rest_pack(j, unused):
        pack(j)
        send_halo(j, AUX)
        return unused

    lax.fori_loop(1, PIECES, rest_pack, 0)

    def spread(value):
        return jnp.broadcast_to(value.reshape(1, NB), (NB, NB)).T

    own_class = classes[...].reshape(1, NB)
    bins = lax.broadcasted_iota(jnp.int32, (1, NB), 1)

    def lookup(table):
        value = jnp.zeros((1, NB), jnp.float32)
        for k in range(NCLS):
            value = jnp.where(own_class == k, table[k], value)
        return value

    rate = step_duration * lookup(break_table)
    sinks[...] = spread(settle[...])
    tables[0] = spread(lookup(up_table))
    tables[1] = spread(lookup(down_table))
    tables[2] = spread(rate / jnp.maximum(bins, 1).astype(jnp.float32))
    tables[3] = spread(jnp.where(bins >= 1, 1.0 - rate, 1.0))

    def weights(spot, along, across, mask):
        factors[spot, 0] = (1.0 - 4.0 * h_diffusion) * mask
        factors[spot, 1] = mask * (h_diffusion - 0.5 * along)
        factors[spot, 2] = mask * (h_diffusion + 0.5 * along)
        factors[spot, 3] = mask * (h_diffusion - 0.5 * across)
        factors[spot, 4] = mask * (h_diffusion + 0.5 * across)

    for r in range(4):
        weights(1 + r, *[rows[r] for rows in fields])
    take_halo(0, 0)
    weights(0, *[down_in[0, k] for k in range(AUX)])
    weights(5, *[up_in[0, k] for k in range(AUX)])

    def transport(west, cells, east, spot):
        swapped = jnp.where(seam, turn(cells, 4, 0), 0.0)
        north = turn(jnp.where(lane_first, swapped, cells), -1, 1)
        south = turn(jnp.where(lane_last, swapped, cells), 1, 1)
        return (
            factors[spot, 0] * cells
            + factors[spot, 1] * east
            + factors[spot, 2] * west
            + factors[spot, 3] * north
            + factors[spot, 4] * south
        )

    def horizontal(j, unused):
        pl.when(j > 0)(lambda: take_halo(j, AUX))
        for n, d in enumerate(OFFSETS):
            for q in range(QUADS):
                spot = AUX + (n * QUADS + q) * 2
                rows = [
                    ref[j, spot + i] for ref in (down_in, up_out, down_out, up_in) for i in (0, 1)
                ]
                once = [transport(*rows[r : r + 3], r) for r in range(6)]
                for r in range(4):
                    twice = transport(*once[r : r + 3], 1 + r)
                    if d:
                        moved[d, j * PART + 4 * q + r] = twice
                    else:
                        column[2 + x, j * PART + 4 * q + r] = twice
            if d:
                ring(j, d).start()
        return unused

    lax.fori_loop(0, PIECES, horizontal, 0)
    pl.when(~bottom)(lambda: pl.semaphore_wait(enter_sem, 1))

    def forward(j):
        for d in (1, 2, 3):
            ring(j, d).wait_recv()
        pl.when(~top)(lambda: deep_up(j).start())
        pl.when(~bottom)(lambda: deep_down(j).start())

    def settle_mix(levels, sink, start):
        share = v_diffusion
        keep, fall = 1.0 - 2.0 * share - sink, share + sink
        fresh = []
        for k in range(len(levels) - 2):
            upper, own, lower = levels[k : k + 3]
            upper_term = fall * upper
            lower_term = share * lower
            if start + k == 2:
                upper_term = jnp.where(top, share * own, upper_term)
            if start + k == 5:
                lower_term = jnp.where(bottom, share * own, lower_term)
            fresh.append(keep * own + upper_term + lower_term)
        return fresh

    def vertical(j):
        pl.when(~top)(lambda: deep_down(j).wait_recv())
        pl.when(~bottom)(lambda: deep_up(j).wait_recv())
        sink = sinks[pl.ds(pl.multiple_of(x * GROUP + j * PART, PART), PART)]
        other = turn(sink, 4, 0)
        for q in range(QUADS):
            own_sink = jnp.where(half, sink, other) if q == 0 else jnp.where(half, other, sink)
            spot = j * PART + 4 * q
            rows = []
            for r in range(4):
                levels = [column[k, spot + r] for k in range(8)]
                rows.append(settle_mix(settle_mix(levels, own_sink, 1), own_sink, 2))
            for k in range(RING):
                for i, cells in enumerate(swap_rows(*[levels[k] for levels in rows])):
                    mixed[k, spot + i] = cells
        for d in (2, 1, 3):
            back(j, d).start()
        for i in range(PART):
            settled[x, j * PART + i] = mixed[x, j * PART + i]

    forward(0)

    def middle(j, unused):
        forward(j)
        vertical(j - 1)
        return unused

    lax.fori_loop(1, PIECES, middle, 0)
    vertical(PIECES - 1)

    def drain(j, unused):
        for d in (1, 2, 3):
            back(j, d).wait_recv()
            ring(j, d).wait_send()
            back(j, d).wait_send()
        pl.when(~top)(lambda: deep_up(j).wait_send())
        pl.when(~bottom)(lambda: deep_down(j).wait_send())
        return unused

    def drain_halo(j, start):
        pl.when(~first_band)(lambda: halo_up(j, start).wait_send())
        pl.when(~last_band)(lambda: halo_down(j, start).wait_send())

    lax.fori_loop(0, PIECES, drain, 0)
    for j in range(PIECES):
        drain_halo(j, 0 if j == 0 else AUX)


def collide_kernel(settled, tables, out, sums):
    parts = NB // PART

    def row(k, b):
        return jnp.broadcast_to(tables[k, pl.ds(b, 1)], (SUB, LANE))

    def total(p, unused):
        b = p * PART
        cells = [settled[b + i] for i in range(PART)]
        for k in range(3):
            terms = [row(k, b + i) * cells[i] for i in range(PART)]
            while len(terms) > 1:
                terms = [one + two for one, two in zip(terms[::2], terms[1::2])]
            sums[k, p] = terms[0]
        return unused

    lax.fori_loop(0, parts, total, 0, unroll=2)
    lower = jnp.zeros((SUB, LANE), jnp.float32)
    for p in range(parts):
        own = sums[0, p]
        sums[0, p] = lower
        lower = lower + own
    for k in (1, 2):
        higher = jnp.zeros((SUB, LANE), jnp.float32)
        for p in reversed(range(parts)):
            higher = higher + sums[k, p]
            sums[k, p] = higher

    def collide(p, unused):
        lower, higher, pieces = sums[0, p], sums[1, p], sums[2, p]
        for i in range(PART):
            b = p * PART + i
            cells = settled[b]
            loss, gain = row(0, b), row(1, b)
            higher = higher - gain * cells
            pieces = pieces - row(2, b) * cells
            out[b] = cells * (row(3, b) + ALPHA * (gain * lower - loss * higher)) + pieces
            lower = lower + loss * cells
        return unused

    lax.fori_loop(0, parts, collide, 0, unroll=2)


def local(depth, bands, conc, *rest):
    cells = conc.reshape(NB, 4, 2, LANE).transpose(0, 2, 1, 3).reshape(NB, SUB, LANE)
    vmem = pl.BlockSpec(memory_space=pltpu.VMEM)
    dma = pltpu.SemaphoreType.DMA
    tile = (SUB, LANE)

    def buffer(*shape):
        return pltpu.VMEM(shape + tile, jnp.float32)

    settled, tables = pl.pallas_call(
        functools.partial(step_kernel, depth, bands),
        out_shape=(
            jax.ShapeDtypeStruct((RING, GROUP) + tile, jnp.float32),
            jax.ShapeDtypeStruct((4, NB, LANE), jnp.float32),
        ),
        in_specs=[pl.BlockSpec(memory_space=pltpu.HBM)] * 9,
        out_specs=(vmem, vmem),
        scratch_shapes=[
            buffer(NB),
            pltpu.VMEM((1, 4, 2 * LANE), jnp.float32),
            pltpu.VMEM((1, 4, 2 * LANE), jnp.float32),
            pltpu.VMEM((4, 2 * LANE), jnp.int32),
            pltpu.VMEM((NB,), jnp.float32),
            pltpu.VMEM((NB,), jnp.int32),
            pltpu.SMEM((NCLS,), jnp.float32),
            pltpu.SMEM((NCLS,), jnp.float32),
            pltpu.SMEM((NCLS,), jnp.float32),
            buffer(PIECES, MESSAGE),
            buffer(PIECES, MESSAGE),
            buffer(PIECES, MESSAGE),
            buffer(PIECES, MESSAGE),
            buffer(RING, GROUP),
            buffer(8, GROUP),
            buffer(RING, GROUP),
            pltpu.VMEM((NB, LANE), jnp.float32),
            buffer(6, 5),
            dma((9,)),
            pltpu.SemaphoreType.REGULAR,
            dma((PIECES,)),
            dma((PIECES,)),
            dma((PIECES,)),
            dma((PIECES,)),
            dma((PIECES, RING)),
            dma((PIECES, RING)),
            dma((PIECES, 2)),
            dma((PIECES, 2)),
            dma((PIECES, RING)),
            dma((PIECES, RING)),
        ],
        compiler_params=pltpu.CompilerParams(
            collective_id=0, has_side_effects=True, vmem_limit_bytes=20 << 20
        ),
    )(cells, *rest)
    result = pl.pallas_call(
        collide_kernel,
        out_shape=jax.ShapeDtypeStruct((NB,) + tile, jnp.float32),
        in_specs=[vmem, vmem],
        out_specs=vmem,
        scratch_shapes=[buffer(3, NB // PART)],
        compiler_params=pltpu.CompilerParams(vmem_limit_bytes=8 << 20),
    )(settled.reshape((NB,) + tile), tables)
    return result.reshape(NB, 2, 4, LANE).transpose(0, 2, 1, 3).reshape(conc.shape)


def solution(mesh):
    placed = (
        P("bins", None, "xy", None),
        P("bins", "xy", None),
        P("bins", "xy", None),
        P("xy", None),
        P(),
        P(),
        P(),
        P(),
        P(),
    )
    return jax.shard_map(
        functools.partial(local, mesh.shape["bins"] // RING, mesh.shape["xy"]),
        mesh=mesh,
        in_specs=placed,
        out_specs=P("bins", None, "xy", None),
        check_vma=False,
    )
```

time: 42 us -> 35.2 us (0.84)
  the two profiles are of different devices: /device:TPU:56 before, /device:TPU:160 now
where the time goes in v3:
time: 35.2 us; the launch traced here: 35 us
  Pallas kernels  29.8 us (85%)
  local copies, waits for them, and re-layouts  5.09 us (14%)
    pallas_call x1, Pallas kernels, local(): pl.pallas_call(functools.partial(step_kernel, depth, bands), out_shape=(j...  28.6 us
    unnamed x18, local copies, waits for them, and re-layouts  5.09 us
    pallas_call x1, Pallas kernels, local(): pl.pallas_call(collide_kernel, out_shape=jax.ShapeDtypeStruct((NB,) + til...  1.26 us

profile of v3, /device:TPU:160, one launch (start us, length us, event | category | flops | bytes accessed | tf_op | source)
XLA Modules:
  0.0 35.0 jit_solution(13556879085510198770)
XLA Ops:
  0.0 0.0 copy-start.6
  0.0 0.0 copy-start.5
  0.0 0.0 copy-start.4
  0.0 0.6 %copy-done.6 = f32[8]{0:T(128)S(1)} copy-done((f32[8]{0:T(128)S(1)}, f32[8]{0:T(128)}, u32[]{:S(2)}) %copy-start.6) | copy-done | bytes 56
  0.7 0.0 copy-done.5
  0.7 0.0 copy-done.4
  0.7 0.0 copy-start
  0.7 1.0 %copy-done = f32[1,128,4,256]{3,2,1,0:T(4,128)S(1)} copy-done((f32[1,128,4,256]{3,2,1,0:T(4,128)S(1)}, f32[1,128,4,256]{3,2,1,0:T(4,128)}, u32[]{:S(2)}) %copy-start) | copy-done | bytes 524312
  1.7 0.0 copy-start.1
  1.7 0.7 %copy-done.1 = f32[1,4,256]{2,1,0:T(4,128)S(1)} copy-done((f32[1,4,256]{2,1,0:T(4,128)S(1)}, f32[1,4,256]{2,1,0:T(4,128)}, u32[]{:S(2)}) %copy-start.1) | copy-done | bytes 4120
  2.4 0.0 copy-start.2
  2.4 0.7 %copy-done.2 = f32[1,4,256]{2,1,0:T(4,128)S(1)} copy-done((f32[1,4,256]{2,1,0:T(4,128)S(1)}, f32[1,4,256]{2,1,0:T(4,128)}, u32[]{:S(2)}) %copy-start.2) | copy-done | bytes 4120
  3.1 0.0 copy-start.3
  3.1 0.7 %copy-done.3 = s32[4,256]{1,0:T(4,128)S(1)} copy-done((s32[4,256]{1,0:T(4,128)S(1)}, s32[4,256]{1,0:T(4,128)}, u32[]{:S(2)}) %copy-start.3) | copy-done | bytes 4120
  3.8 0.0 copy-start.7
  3.8 0.7 %copy-done.7 = f32[8]{0:T(128)S(1)} copy-done((f32[8]{0:T(128)S(1)}, f32[8]{0:T(128)}, u32[]{:S(2)}) %copy-start.7) | copy-done | bytes 56
  4.4 0.0 copy-start.8
  4.5 0.7 %copy-done.8 = f32[8]{0:T(128)S(1)} copy-done((f32[8]{0:T(128)S(1)}, f32[8]{0:T(128)}, u32[]{:S(2)}) %copy-start.8) | copy-done | bytes 56
  5.1 28.6 %shard_map.91 = (f32[4,32,8,128]{3,2,1,0:T(8,128)S(1)}, f32[4,128,128]{2,1,0:T(8,128)S(1)}) custom-call(f32[128,8,128]{2,1,0:T(8,128)S(1)} %bitcast.11, f32[1,4,256]{2,1,0:T(4,128)S(1)} %copy-done.1, f32[1,4,256]{2,1,0:T(4,128)S(1)} %copy-done.2, s32[4,256]{1,0:T(4,128)S(1)} %copy-done.3, f32[128]{0:T(128)S(1)} %copy-done.4, s32[128]{0:T(128)S(1)} %copy-done.5, ...), custom_call_target="tpu_custom_call" | custom-call | tf_op jit(solution)/shard_map/pallas_call | solution.py:445
  33.7 1.3 %shard_map.92 = f32[128,8,128]{2,1,0:T(8,128)} custom-call(f32[128,8,128]{2,1,0:T(8,128)S(1)} %bitcast.12, f32[4,128,128]{2,1,0:T(8,128)S(1)} %get-tuple-element.8.tables), custom_call_target="tpu_custom_call" | custom-call | tf_op jit(solution)/shard_map/pallas_call | solution.py:489
Async XLA Ops:
  0.0 0.7 %copy-start.6 = (f32[8]{0:T(128)S(1)}, f32[8]{0:T(128)}, u32[]{:S(2)}) copy-start(f32[8]{0:T(128)} %up_hbm.1) | copy-start | bytes 100
  0.0 0.7 %copy-start.5 = (s32[128]{0:T(128)S(1)}, s32[128]{0:T(128)}, u32[]{:S(2)}) copy-start(s32[128]{0:T(128)} %classes_hbm.1) | copy-start | bytes 1540
  0.0 0.7 %copy-start.4 = (f32[128]{0:T(128)S(1)}, f32[128]{0:T(128)}, u32[]{:S(2)}) copy-start(f32[128]{0:T(128)} %settle_hbm.1) | copy-start | bytes 1540
  0.7 1.0 %copy-start = (f32[1,128,4,256]{3,2,1,0:T(4,128)S(1)}, f32[1,128,4,256]{3,2,1,0:T(4,128)}, u32[]{:S(2)}) copy-start(f32[1,128,4,256]{3,2,1,0:T(4,128)} %param.9) | copy-start | bytes 1572868
  1.7 0.7 %copy-start.1 = (f32[1,4,256]{2,1,0:T(4,128)S(1)}, f32[1,4,256]{2,1,0:T(4,128)}, u32[]{:S(2)}) copy-start(f32[1,4,256]{2,1,0:T(4,128)} %vel_x_hbm.1) | copy-start | bytes 12292
  2.4 0.7 %copy-start.2 = (f32[1,4,256]{2,1,0:T(4,128)S(1)}, f32[1,4,256]{2,1,0:T(4,128)}, u32[]{:S(2)}) copy-start(f32[1,4,256]{2,1,0:T(4,128)} %vel_y_hbm.1) | copy-start | bytes 12292
  3.1 0.7 %copy-start.3 = (s32[4,256]{1,0:T(4,128)S(1)}, s32[4,256]{1,0:T(4,128)}, u32[]{:S(2)}) copy-start(s32[4,256]{1,0:T(4,128)} %sea_mask_hbm.1) | copy-start | bytes 12292
  3.8 0.7 %copy-start.7 = (f32[8]{0:T(128)S(1)}, f32[8]{0:T(128)}, u32[]{:S(2)}) copy-start(f32[8]{0:T(128)} %down_hbm.1) | copy-start | bytes 100
  4.4 0.7 %copy-start.8 = (f32[8]{0:T(128)S(1)}, f32[8]{0:T(128)}, u32[]{:S(2)}) copy-start(f32[8]{0:T(128)} %break_hbm.1) | copy-start | bytes 100

commit v4 on v3

--- a/solution.py
+++ b/solution.py
@@ -24,12 +24,27 @@
 QUADS = PART // 4
 OFFSETS = (2, 1, 3, 0)
 AUX = 3
-MESSAGE = AUX + RING * QUADS * 2
+SPAN = 8
+BATCH = RING * QUADS * 2
+MESSAGE = AUX + PIECES * BATCH
 ALPHA = step_duration * collide_scale / NB
 
 
 def turn(value, shift, axis):
     return pltpu.roll(value, shift % value.shape[axis], axis)
+
+
+def swap_rows(a, b, c, d):
+    sub = lax.broadcasted_iota(jnp.int32, (SUB, LANE), 0)
+    even, low = sub % 2 == 0, sub % 4 < 2
+    ab, ba = jnp.where(even, a, turn(b, 1, 0)), jnp.where(even, turn(a, -1, 0), b)
+    cd, dc = jnp.where(even, c, turn(d, 1, 0)), jnp.where(even, turn(c, -1, 0), d)
+    return (
+        jnp.where(low, ab, turn(cd, 2, 0)),
+        jnp.where(low, ba, turn(dc, 2, 0)),
+        jnp.where(low, turn(ab, -2, 0), cd),
+        jnp.where(low, turn(ba, -2, 0), dc),
+    )
 
 
 def step_kernel(
@@ -124,21 +139,9 @@
 
     sub = lax.broadcasted_iota(jnp.int32, (SUB, LANE), 0)
     lane = lax.broadcasted_iota(jnp.int32, (SUB, LANE), 1)
-    even = sub % 2 == 0
-    low = sub % 4 < 2
     lane_first, lane_last = lane == 0, lane == LANE - 1
     half = sub < 4
     seam = (half & lane_first) | (~half & lane_last)
-
-    def swap_rows(a, b, c, d):
-        ab, ba = jnp.where(even, a, turn(b, 1, 0)), jnp.where(even, turn(a, -1, 0), b)
-        cd, dc = jnp.where(even, c, turn(d, 1, 0)), jnp.where(even, turn(c, -1, 0), d)
-        return (
-            jnp.where(low, ab, turn(cd, 2, 0)),
-            jnp.where(low, ba, turn(dc, 2, 0)),
-            jnp.where(low, turn(ab, -2, 0), cd),
-            jnp.where(low, turn(ba, -2, 0), dc),
-        )
 
     for copy in loads:
         copy.wait()
@@ -152,46 +155,44 @@
         for value in (plane(vel_x), plane(vel_y), plane(sea_mask).astype(jnp.float32))
     ]
     for k, rows in enumerate(fields):
-        up_out[0, k] = rows[0]
-        down_out[0, k] = rows[3]
+        up_out[k] = rows[0]
+        down_out[k] = rows[3]
 
     def pack(j):
         for n, d in enumerate(OFFSETS):
             for q in range(QUADS):
                 first = (x + d) % RING * GROUP + j * PART + 4 * q
                 rows = swap_rows(*[conc[first + i] for i in range(4)])
-                spot = AUX + (n * QUADS + q) * 2
-                up_out[j, spot], up_out[j, spot + 1] = rows[0], rows[1]
-                down_out[j, spot], down_out[j, spot + 1] = rows[2], rows[3]
+                spot = AUX + j * BATCH + (n * QUADS + q) * 2
+                up_out[spot], up_out[spot + 1] = rows[0], rows[1]
+                down_out[spot], down_out[spot + 1] = rows[2], rows[3]
+
+    def halo(j, start, source, target, send, recv, to):
+        rows = pl.ds(start + j * BATCH, BATCH + AUX - start)
+        return pltpu.make_async_remote_copy(
+            src_ref=source.at[rows],
+            dst_ref=target.at[rows],
+            send_sem=send,
+            recv_sem=recv.at[j],
+            device_id=(place, to),
+            device_id_type=MESH,
+        )
 
     def halo_up(j, start):
-        rows = pl.ds(start, MESSAGE - start)
-        return pltpu.make_async_remote_copy(
-            src_ref=up_out.at[j, rows],
-            dst_ref=up_in.at[j, rows],
-            send_sem=up_send.at[j],
-            recv_sem=up_recv.at[j],
-            device_id=(place, band - 1),
-            device_id_type=MESH,
-        )
+        return halo(j, start, up_out, up_in, up_send, up_recv, band - 1)
 
     def halo_down(j, start):
-        rows = pl.ds(start, MESSAGE - start)
-        return pltpu.make_async_remote_copy(
-            src_ref=down_out.at[j, rows],
-            dst_ref=down_in.at[j, rows],
-            send_sem=down_send.at[j],
-            recv_sem=down_recv.at[j],
-            device_id=(place, band + 1),
-            device_id_type=MESH,
-        )
+        return halo(j, start, down_out, down_in, down_send, down_recv, band + 1)
+
+    def settle_bytes(ref, sem):
+        pltpu.make_async_copy(ref, ref, sem).wait()
 
     def ring(j, d):
         return pltpu.make_async_remote_copy(
             src_ref=moved.at[d, pl.ds(j * PART, PART)],
             dst_ref=column.at[2 + x, pl.ds(j * PART, PART)],
-            send_sem=ring_send.at[j, d],
-            recv_sem=ring_recv.at[j, d],
+            send_sem=ring_send,
+            recv_sem=ring_recv.at[j],
             device_id=(z * RING + (x + d) % RING, band),
             device_id_type=MESH,
         )
@@ -201,7 +202,7 @@
         return pltpu.make_async_remote_copy(
             src_ref=column.at[pl.ds(4, 2), part],
             dst_ref=column.at[pl.ds(0, 2), part],
-            send_sem=deep_send.at[j, 0],
+            send_sem=deep_send.at[0],
             recv_sem=deep_recv.at[j, 0],
             device_id=(place + RING, band),
             device_id_type=MESH,
@@ -212,20 +213,20 @@
         return pltpu.make_async_remote_copy(
             src_ref=column.at[pl.ds(2, 2), part],
             dst_ref=column.at[pl.ds(6, 2), part],
-            send_sem=deep_send.at[j, 1],
+            send_sem=deep_send.at[1],
             recv_sem=deep_recv.at[j, 1],
             device_id=(place - RING, band),
             device_id_type=MESH,
         )
 
-    def back(j, d):
+    def back(j, level, source):
         part = pl.ds(j * PART, PART)
         return pltpu.make_async_remote_copy(
-            src_ref=mixed.at[(x + d) % RING, part],
-            dst_ref=settled.at[x, part],
-            send_sem=back_send.at[j, d],
-            recv_sem=back_recv.at[j, d],
-            device_id=(z * RING + (x + d) % RING, band),
+            src_ref=mixed.at[level, part],
+            dst_ref=settled.at[source, part],
+            send_sem=back_send,
+            recv_sem=back_recv,
+            device_id=(z * RING + level, band),
             device_id_type=MESH,
         )
 
@@ -268,7 +269,12 @@
         return value
 
     rate = step_duration * lookup(break_table)
-    sinks[...] = spread(settle[...])
+    tables[0] = spread(settle[...])
+    for k in range(GROUP // SUB):
+        sink = tables[0, pl.ds(pl.multiple_of(x * GROUP + k * SUB, SUB), SUB)]
+        other = turn(sink, 4, 0)
+        sinks[2 * k] = jnp.where(half, sink, other)
+        sinks[2 * k + 1] = jnp.where(half, other, sink)
     tables[0] = spread(lookup(up_table))
     tables[1] = spread(lookup(down_table))
     tables[2] = spread(rate / jnp.maximum(bins, 1).astype(jnp.float32))
@@ -284,8 +290,8 @@
     for r in range(4):
         weights(1 + r, *[rows[r] for rows in fields])
     take_halo(0, 0)
-    weights(0, *[down_in[0, k] for k in range(AUX)])
-    weights(5, *[up_in[0, k] for k in range(AUX)])
+    weights(0, *[down_in[k] for k in range(AUX)])
+    weights(5, *[up_in[k] for k in range(AUX)])
 
     def transport(west, cells, east, spot):
         swapped = jnp.where(seam, turn(cells, 4, 0), 0.0)
@@ -303,9 +309,9 @@
         pl.when(j > 0)(lambda: take_halo(j, AUX))
         for n, d in enumerate(OFFSETS):
             for q in range(QUADS):
-                spot = AUX + (n * QUADS + q) * 2
+                spot = AUX + j * BATCH + (n * QUADS + q) * 2
                 rows = [
-                    ref[j, spot + i] for ref in (down_in, up_out, down_out, up_in) for i in (0, 1)
+                    ref[spot + i] for ref in (down_in, up_out, down_out, up_in) for i in (0, 1)
                 ]
                 once = [transport(*rows[r : r + 3], r) for r in range(6)]
                 for r in range(4):
@@ -314,16 +320,15 @@
                         moved[d, j * PART + 4 * q + r] = twice
                     else:
                         column[2 + x, j * PART + 4 * q + r] = twice
-            if d:
-                ring(j, d).start()
+        for d in OFFSETS[:3]:
+            ring(j, d).start()
         return unused
 
     lax.fori_loop(0, PIECES, horizontal, 0)
     pl.when(~bottom)(lambda: pl.semaphore_wait(enter_sem, 1))
 
     def forward(j):
-        for d in (1, 2, 3):
-            ring(j, d).wait_recv()
+        settle_bytes(column.at[pl.ds(2, 3), pl.ds(j * PART, PART)], ring_recv.at[j])
         pl.when(~top)(lambda: deep_up(j).start())
         pl.when(~bottom)(lambda: deep_down(j).start())
 
@@ -342,65 +347,70 @@
             fresh.append(keep * own + upper_term + lower_term)
         return fresh
 
-    def vertical(j):
-        pl.when(~top)(lambda: deep_down(j).wait_recv())
-        pl.when(~bottom)(lambda: deep_up(j).wait_recv())
-        sink = sinks[pl.ds(pl.multiple_of(x * GROUP + j * PART, PART), PART)]
-        other = turn(sink, 4, 0)
+    def vertical(j, first, wide):
         for q in range(QUADS):
-            own_sink = jnp.where(half, sink, other) if q == 0 else jnp.where(half, other, sink)
             spot = j * PART + 4 * q
+            sink = sinks[j * QUADS + q]
             rows = []
             for r in range(4):
-                levels = [column[k, spot + r] for k in range(8)]
-                rows.append(settle_mix(settle_mix(levels, own_sink, 1), own_sink, 2))
-            for k in range(RING):
-                for i, cells in enumerate(swap_rows(*[levels[k] for levels in rows])):
-                    mixed[k, spot + i] = cells
-        for d in (2, 1, 3):
-            back(j, d).start()
+                levels = [column[first - 2 + k, spot + r] for k in range(wide + 4)]
+                rows.append(settle_mix(settle_mix(levels, sink, first - 1), sink, first))
+            for k in range(wide):
+                for r in range(4):
+                    mixed[first - 2 + k, spot + r] = rows[r][k]
+        for level in range(first - 2, first - 2 + wide):
+            pl.when(x != level)(lambda level=level: back(j, level, x).start())
+
+    def upper_half(j):
+        pl.when(~top)(lambda: deep_down(j).wait_recv())
+        vertical(j, 2, 2)
+
+    def lower_half(j, unused):
+        pl.when(~bottom)(lambda: deep_up(j).wait_recv())
+        vertical(j, 4, 2)
         for i in range(PART):
             settled[x, j * PART + i] = mixed[x, j * PART + i]
+        return unused
 
     forward(0)
 
     def middle(j, unused):
         forward(j)
-        vertical(j - 1)
+        upper_half(j - 1)
         return unused
 
     lax.fori_loop(1, PIECES, middle, 0)
-    vertical(PIECES - 1)
-
-    def drain(j, unused):
-        for d in (1, 2, 3):
-            back(j, d).wait_recv()
-            ring(j, d).wait_send()
-            back(j, d).wait_send()
-        pl.when(~top)(lambda: deep_up(j).wait_send())
-        pl.when(~bottom)(lambda: deep_down(j).wait_send())
-        return unused
-
-    def drain_halo(j, start):
-        pl.when(~first_band)(lambda: halo_up(j, start).wait_send())
-        pl.when(~last_band)(lambda: halo_down(j, start).wait_send())
-
-    lax.fori_loop(0, PIECES, drain, 0)
-    for j in range(PIECES):
-        drain_halo(j, 0 if j == 0 else AUX)
-
-
-def collide_kernel(settled, tables, out, sums):
-    parts = NB // PART
+    upper_half(PIECES - 1)
+    lax.fori_loop(0, PIECES, lower_half, 0)
+
+    settle_bytes(settled.at[pl.ds(0, 3)], back_recv)
+    settle_bytes(moved.at[pl.ds(1, 3)], ring_send)
+    settle_bytes(mixed.at[pl.ds(0, 3)], back_send)
+    pl.when(~top)(lambda: settle_bytes(column.at[pl.ds(2, 2)], deep_send.at[1]))
+    pl.when(~bottom)(lambda: settle_bytes(column.at[pl.ds(4, 2)], deep_send.at[0]))
+    pl.when(~first_band)(lambda: settle_bytes(up_out, up_send))
+    pl.when(~last_band)(lambda: settle_bytes(down_out, down_send))
+
+
+def collide_kernel(settled, tables, out_hbm, cells_by_bin, out, sums, out_sem):
+    parts = NB // SPAN
 
     def row(k, b):
         return jnp.broadcast_to(tables[k, pl.ds(b, 1)], (SUB, LANE))
 
+    def store(p):
+        part = pl.ds(p * SPAN, SPAN)
+        return pltpu.make_async_copy(out.at[part], out_hbm.at[part], out_sem.at[p])
+
     def total(p, unused):
-        b = p * PART
-        cells = [settled[b + i] for i in range(PART)]
+        b = p * SPAN
+        cells = []
+        for q in range(0, SPAN, 4):
+            cells += swap_rows(*[settled[b + q + r] for r in range(4)])
+        for i in range(SPAN):
+            cells_by_bin[b + i] = cells[i]
         for k in range(3):
-            terms = [row(k, b + i) * cells[i] for i in range(PART)]
+            terms = [row(k, b + i) * cells[i] for i in range(SPAN)]
             while len(terms) > 1:
                 terms = [one + two for one, two in zip(terms[::2], terms[1::2])]
             sums[k, p] = terms[0]
@@ -420,17 +430,24 @@
 
     def collide(p, unused):
         lower, higher, pieces = sums[0, p], sums[1, p], sums[2, p]
-        for i in range(PART):
-            b = p * PART + i
-            cells = settled[b]
+        for i in range(SPAN):
+            b = p * SPAN + i
+            cells = cells_by_bin[b]
             loss, gain = row(0, b), row(1, b)
             higher = higher - gain * cells
             pieces = pieces - row(2, b) * cells
             out[b] = cells * (row(3, b) + ALPHA * (gain * lower - loss * higher)) + pieces
             lower = lower + loss * cells
+        store(p).start()
         return unused
 
     lax.fori_loop(0, parts, collide, 0, unroll=2)
+
+    def finish(p, unused):
+        store(p).wait()
+        return unused
+
+    lax.fori_loop(0, parts, finish, 0)
 
 
 def local(depth, bands, conc, *rest):
@@ -460,38 +477,38 @@
             pltpu.SMEM((NCLS,), jnp.float32),
             pltpu.SMEM((NCLS,), jnp.float32),
             pltpu.SMEM((NCLS,), jnp.float32),
-            buffer(PIECES, MESSAGE),
-            buffer(PIECES, MESSAGE),
-            buffer(PIECES, MESSAGE),
-            buffer(PIECES, MESSAGE),
+            buffer(MESSAGE),
+            buffer(MESSAGE),
+            buffer(MESSAGE),
+            buffer(MESSAGE),
             buffer(RING, GROUP),
             buffer(8, GROUP),
             buffer(RING, GROUP),
-            pltpu.VMEM((NB, LANE), jnp.float32),
+            buffer(GROUP // 4),
             buffer(6, 5),
             dma((9,)),
             pltpu.SemaphoreType.REGULAR,
+            dma,
             dma((PIECES,)),
+            dma,
             dma((PIECES,)),
+            dma,
             dma((PIECES,)),
-            dma((PIECES,)),
-            dma((PIECES, RING)),
-            dma((PIECES, RING)),
+            dma((2,)),
             dma((PIECES, 2)),
-            dma((PIECES, 2)),
-            dma((PIECES, RING)),
-            dma((PIECES, RING)),
+            dma,
+            dma,
         ],
         compiler_params=pltpu.CompilerParams(
             collective_id=0, has_side_effects=True, vmem_limit_bytes=20 << 20
         ),
-    )(cells, *rest)
+    )(*[pltpu.with_memory_space_constraint(value, pltpu.HBM) for value in (cells, *rest)])
     result = pl.pallas_call(
         collide_kernel,
         out_shape=jax.ShapeDtypeStruct((NB,) + tile, jnp.float32),
         in_specs=[vmem, vmem],
-        out_specs=vmem,
-        scratch_shapes=[buffer(3, NB // PART)],
+        out_specs=pl.BlockSpec(memory_space=pl.ANY),
+        scratch_shapes=[buffer(NB), buffer(NB), buffer(3, NB // SPAN), dma((NB // SPAN,))],
         compiler_params=pltpu.CompilerParams(vmem_limit_bytes=8 << 20),
     )(settled.reshape((NB,) + tile), tables)
     return result.reshape(NB, 2, 4, LANE).transpose(0, 2, 1, 3).reshape(conc.shape)

time: 35.2 us -> 27.9 us (0.79)
  the two profiles are of different devices: /device:TPU:160 before, /device:TPU:71 now
where the time goes in v4:
time: 27.9 us; the launch traced here: 27.8 us
  Pallas kernels  27.8 us (100%)
    pallas_call x1, Pallas kernels, local(): pl.pallas_call(functools.partial(step_kernel, depth, bands), out_shape=(j...  26.5 us
    pallas_call x1, Pallas kernels, local(): pl.pallas_call(collide_kernel, out_shape=jax.ShapeDtypeStruct((NB,) + til...  1.29 us

profile of v4, /device:TPU:71, one launch (start us, length us, event | category | flops | bytes accessed | tf_op | source)
XLA Modules:
  0.0 27.8 jit_solution(2263662635070712696)
XLA Ops:
  0.0 26.5 %shard_map.91 = (f32[4,32,8,128]{3,2,1,0:T(8,128)S(1)}, f32[4,128,128]{2,1,0:T(8,128)S(1)}) custom-call(f32[128,8,128]{2,1,0:T(8,128)} %bitcast.12, f32[1,4,256]{2,1,0:T(4,128)} %vel_x_hbm.1, f32[1,4,256]{2,1,0:T(4,128)} %vel_y_hbm.1, s32[4,256]{1,0:T(4,128)} %sea_mask_hbm.1, f32[128]{0:T(128)} %settle_hbm.1, s32[128]{0:T(128)} %classes_hbm.1, f32[8]{0:T(128)} %up_hbm.1, ...), custom_call_target="tpu_custom_call" | custom-call | tf_op jit(solution)/shard_map/pallas_call | solution.py:462
  26.5 1.3 %shard_map.92 = f32[128,8,128]{2,1,0:T(8,128)} custom-call(f32[128,8,128]{2,1,0:T(8,128)S(1)} %bitcast.11, f32[4,128,128]{2,1,0:T(8,128)S(1)} %get-tuple-element.8.tables), custom_call_target="tpu_custom_call" | custom-call | tf_op jit(solution)/shard_map/pallas_call | solution.py:506

commit v5 on v4

--- a/solution.py
+++ b/solution.py
@@ -19,7 +19,7 @@
 SUB, LANE = 8, 128
 RING = 4
 GROUP = NB // RING
-PIECES = 4
+PIECES = 8
 PART = GROUP // PIECES
 QUADS = PART // 4
 OFFSETS = (2, 1, 3, 0)
@@ -365,23 +365,29 @@
         pl.when(~top)(lambda: deep_down(j).wait_recv())
         vertical(j, 2, 2)
 
-    def lower_half(j, unused):
+    def lower_half(j):
         pl.when(~bottom)(lambda: deep_up(j).wait_recv())
         vertical(j, 4, 2)
         for i in range(PART):
             settled[x, j * PART + i] = mixed[x, j * PART + i]
-        return unused
-
-    forward(0)
-
-    def middle(j, unused):
-        forward(j)
-        upper_half(j - 1)
-        return unused
-
-    lax.fori_loop(1, PIECES, middle, 0)
-    upper_half(PIECES - 1)
-    lax.fori_loop(0, PIECES, lower_half, 0)
+
+    def follow(lead, lag):
+        for j in range(lead):
+            forward(j)
+        for j in range(PIECES + lag):
+            if j < PIECES:
+                upper_half(j)
+            if j >= lag:
+                lower_half(j - lag)
+            if lead + j < PIECES:
+                forward(lead + j)
+
+    corner = band < 2
+    together = (z > depth // 2) | (top & corner)
+    apart = ~together & ~((z == 1) & corner)
+    pl.when(together)(lambda: follow(5, 0))
+    pl.when(apart)(lambda: follow(5, 4))
+    pl.when(~together & ~apart)(lambda: follow(PIECES, 0))
 
     settle_bytes(settled.at[pl.ds(0, 3)], back_recv)
     settle_bytes(moved.at[pl.ds(1, 3)], ring_send)

time: 27.9 us -> 26 us (0.932)
  the two profiles are of different devices: /device:TPU:71 before, /device:TPU:1 now
where the time goes in v5:
time: 26 us; the launch traced here: 25.9 us
  Pallas kernels  25.8 us (99%)
    pallas_call x1, Pallas kernels, local(): pl.pallas_call(functools.partial(step_kernel, depth, bands), out_shape=(j...  24.6 us
    pallas_call x1, Pallas kernels, local(): pl.pallas_call(collide_kernel, out_shape=jax.ShapeDtypeStruct((NB,) + til...  1.29 us

profile of v5, /device:TPU:1, one launch (start us, length us, event | category | flops | bytes accessed | tf_op | source)
XLA Modules:
  0.0 25.9 jit_solution(4329794004284582351)
XLA Ops:
  0.0 24.6 %shard_map.91 = (f32[4,32,8,128]{3,2,1,0:T(8,128)S(1)}, f32[4,128,128]{2,1,0:T(8,128)S(1)}) custom-call(f32[128,8,128]{2,1,0:T(8,128)} %bitcast.12, f32[1,4,256]{2,1,0:T(4,128)} %vel_x_hbm.1, f32[1,4,256]{2,1,0:T(4,128)} %vel_y_hbm.1, s32[4,256]{1,0:T(4,128)} %sea_mask_hbm.1, f32[128]{0:T(128)} %settle_hbm.1, s32[128]{0:T(128)} %classes_hbm.1, f32[8]{0:T(128)} %up_hbm.1, ...), custom_call_target="tpu_custom_call" | custom-call | tf_op jit(solution)/shard_map/pallas_call | solution.py:468
  24.6 1.3 %shard_map.92 = f32[128,8,128]{2,1,0:T(8,128)} custom-call(f32[128,8,128]{2,1,0:T(8,128)S(1)} %bitcast.11, f32[4,128,128]{2,1,0:T(8,128)S(1)} %get-tuple-element.8.tables), custom_call_target="tpu_custom_call" | custom-call | tf_op jit(solution)/shard_map/pallas_call | solution.py:512

commit v6 on v5

--- a/solution.py
+++ b/solution.py
@@ -81,6 +81,7 @@
     factors,
     load_sem,
     enter_sem,
+    higher_sem,
     up_send,
     up_recv,
     down_send,
@@ -102,10 +103,10 @@
     def greet(bins, xy):
         pl.semaphore_signal(barrier, inc=1, device_id=(bins, xy), device_id_type=MESH)
 
-    for d in (1, 2, 3):
-        greet(z * RING + (x + d) % RING, band)
     pl.when(~first_band)(lambda: greet(place, band - 1))
     pl.when(~last_band)(lambda: greet(place, band + 1))
+    for d in (1, 2, 3):
+        pl.when(x < RING - d)(lambda d=d: greet(place + d, band))
     pl.when(~bottom)(lambda: greet(place + RING, band))
 
     loads = [
@@ -239,7 +240,7 @@
         pl.when(~first_band)(lambda: halo_down(j, start).wait_recv())
 
     pack(0)
-    greeted = 3 + (1 - first_band.astype(jnp.int32)) + (1 - last_band.astype(jnp.int32))
+    greeted = x + (1 - first_band.astype(jnp.int32)) + (1 - last_band.astype(jnp.int32))
     pl.semaphore_wait(barrier, greeted + (1 - top.astype(jnp.int32)))
     send_halo(0, 0)
 
@@ -248,6 +249,14 @@
         pl.semaphore_signal(
             enter_sem, inc=1, device_id=(place - RING, band), device_id_type=MESH
         )
+
+    for d in (1, 2, 3):
+
+        @pl.when(x >= d)
+        def _(d=d):
+            pl.semaphore_signal(
+                higher_sem, inc=1, device_id=(place - d, band), device_id_type=MESH
+            )
 
     def rest_pack(j, unused):
         pack(j)
@@ -320,6 +329,7 @@
                         moved[d, j * PART + 4 * q + r] = twice
                     else:
                         column[2 + x, j * PART + 4 * q + r] = twice
+        pl.when((j == 0) & (x < RING - 1))(lambda: pl.semaphore_wait(higher_sem, RING - 1 - x))
         for d in OFFSETS[:3]:
             ring(j, d).start()
         return unused
@@ -385,8 +395,8 @@
     corner = band < 2
     together = (z > depth // 2) | (top & corner)
     apart = ~together & ~((z == 1) & corner)
-    pl.when(together)(lambda: follow(5, 0))
-    pl.when(apart)(lambda: follow(5, 4))
+    pl.when(together)(lambda: follow(4, 1))
+    pl.when(apart)(lambda: follow(6, 3))
     pl.when(~together & ~apart)(lambda: follow(PIECES, 0))
 
     settle_bytes(settled.at[pl.ds(0, 3)], back_recv)
@@ -422,7 +432,7 @@
             sums[k, p] = terms[0]
         return unused
 
-    lax.fori_loop(0, parts, total, 0, unroll=2)
+    lax.fori_loop(0, parts, total, 0, unroll=4)
     lower = jnp.zeros((SUB, LANE), jnp.float32)
     for p in range(parts):
         own = sums[0, p]
@@ -447,7 +457,7 @@
         store(p).start()
         return unused
 
-    lax.fori_loop(0, parts, collide, 0, unroll=2)
+    lax.fori_loop(0, parts, collide, 0, unroll=4)
 
     def finish(p, unused):
         store(p).wait()
@@ -494,6 +504,7 @@
             buffer(6, 5),
             dma((9,)),
             pltpu.SemaphoreType.REGULAR,
+            pltpu.SemaphoreType.REGULAR,
             dma,
             dma((PIECES,)),
             dma,

time: 26 us -> 25.1 us (0.965)
  Pallas kernels: 25.8 us -> 25 us
    pallas_call x1, Pallas kernels: 24.6 us -> 23.8 us  [local(): pl.pallas_call(functools.partial(step_kernel, depth, bands), out_shape=(j...]
where the time goes in v6:
time: 25.1 us; the launch traced here: 25 us
  Pallas kernels  25 us (100%)
    pallas_call x1, Pallas kernels, local(): pl.pallas_call(functools.partial(step_kernel, depth, bands), out_shape=(j...  23.8 us
    pallas_call x1, Pallas kernels, local(): pl.pallas_call(collide_kernel, out_shape=jax.ShapeDtypeStruct((NB,) + til...  1.22 us

profile of v6, /device:TPU:1, one launch (start us, length us, event | category | flops | bytes accessed | tf_op | source)
XLA Modules:
  0.0 25.0 jit_solution(1352024869648718563)
XLA Ops:
  0.0 23.8 %shard_map.91 = (f32[4,32,8,128]{3,2,1,0:T(8,128)S(1)}, f32[4,128,128]{2,1,0:T(8,128)S(1)}) custom-call(f32[128,8,128]{2,1,0:T(8,128)} %bitcast.12, f32[1,4,256]{2,1,0:T(4,128)} %vel_x_hbm.1, f32[1,4,256]{2,1,0:T(4,128)} %vel_y_hbm.1, s32[4,256]{1,0:T(4,128)} %sea_mask_hbm.1, f32[128]{0:T(128)} %settle_hbm.1, s32[128]{0:T(128)} %classes_hbm.1, f32[8]{0:T(128)} %up_hbm.1, ...), custom_call_target="tpu_custom_call" | custom-call | tf_op jit(solution)/shard_map/pallas_call | solution.py:478
  23.8 1.2 %shard_map.92 = f32[128,8,128]{2,1,0:T(8,128)} custom-call(f32[128,8,128]{2,1,0:T(8,128)S(1)} %bitcast.11, f32[4,128,128]{2,1,0:T(8,128)S(1)} %get-tuple-element.8.tables), custom_call_target="tpu_custom_call" | custom-call | tf_op jit(solution)/shard_map/pallas_call | solution.py:523

commit v7 on v6

--- a/solution.py
+++ b/solution.py
@@ -25,6 +25,7 @@
 OFFSETS = (2, 1, 3, 0)
 AUX = 3
 SPAN = 8
+AHEAD = 1
 BATCH = RING * QUADS * 2
 MESSAGE = AUX + PIECES * BATCH
 ALPHA = step_duration * collide_scale / NB
@@ -193,7 +194,7 @@
             src_ref=moved.at[d, pl.ds(j * PART, PART)],
             dst_ref=column.at[2 + x, pl.ds(j * PART, PART)],
             send_sem=ring_send,
-            recv_sem=ring_recv.at[j],
+            recv_sem=ring_recv.at[j, x // 2],
             device_id=(z * RING + (x + d) % RING, band),
             device_id_type=MESH,
         )
@@ -337,9 +338,21 @@
     lax.fori_loop(0, PIECES, horizontal, 0)
     pl.when(~bottom)(lambda: pl.semaphore_wait(enter_sem, 1))
 
+    def arrived(j, pair):
+        own = x // 2 == pair
+        for mine, count in ((own, 1), (~own, 2)):
+            part = column.at[pl.ds(2, count), pl.ds(j * PART, PART)]
+            pl.when(mine)(lambda part=part: settle_bytes(part, ring_recv.at[j, pair]))
+
+    def forward_up(j):
+        arrived(j, 0)
+        pl.when(~top)(lambda: deep_up(j).start())
+
     def forward(j):
-        settle_bytes(column.at[pl.ds(2, 3), pl.ds(j * PART, PART)], ring_recv.at[j])
-        pl.when(~top)(lambda: deep_up(j).start())
+        for k in range(AHEAD + 1) if j == 0 else (j + AHEAD,):
+            if k < PIECES:
+                forward_up(k)
+        arrived(j, 1)
         pl.when(~bottom)(lambda: deep_down(j).start())
 
     def settle_mix(levels, sink, start):
@@ -396,7 +409,7 @@
     together = (z > depth // 2) | (top & corner)
     apart = ~together & ~((z == 1) & corner)
     pl.when(together)(lambda: follow(4, 1))
-    pl.when(apart)(lambda: follow(6, 3))
+    pl.when(apart)(lambda: follow(6, 2))
     pl.when(~together & ~apart)(lambda: follow(PIECES, 0))
 
     settle_bytes(settled.at[pl.ds(0, 3)], back_recv)
@@ -510,7 +523,7 @@
             dma,
             dma((PIECES,)),
             dma,
-            dma((PIECES,)),
+            dma((PIECES, 2)),
             dma((2,)),
             dma((PIECES, 2)),
             dma,

time: 25.1 us -> 24.9 us (level)
  no operation moved by 1% of the time
where the time goes in v7:
time: 24.9 us; the launch traced here: 24.8 us
  Pallas kernels  24.8 us (100%)
    pallas_call x1, Pallas kernels, local(): pl.pallas_call(functools.partial(step_kernel, depth, bands), out_shape=(j...  23.5 us
    pallas_call x1, Pallas kernels, local(): pl.pallas_call(collide_kernel, out_shape=jax.ShapeDtypeStruct((NB,) + til...  1.22 us

profile of v7, /device:TPU:1, one launch (start us, length us, event | category | flops | bytes accessed | tf_op | source)
XLA Modules:
  0.0 24.8 jit_solution(15148344289418093774)
XLA Ops:
  0.0 23.5 %shard_map.91 = (f32[4,32,8,128]{3,2,1,0:T(8,128)S(1)}, f32[4,128,128]{2,1,0:T(8,128)S(1)}) custom-call(f32[128,8,128]{2,1,0:T(8,128)} %bitcast.12, f32[1,4,256]{2,1,0:T(4,128)} %vel_x_hbm.1, f32[1,4,256]{2,1,0:T(4,128)} %vel_y_hbm.1, s32[4,256]{1,0:T(4,128)} %sea_mask_hbm.1, f32[128]{0:T(128)} %settle_hbm.1, s32[128]{0:T(128)} %classes_hbm.1, f32[8]{0:T(128)} %up_hbm.1, ...), custom_call_target="tpu_custom_call" | custom-call | tf_op jit(solution)/shard_map/pallas_call | solution.py:491
  23.5 1.2 %shard_map.92 = f32[128,8,128]{2,1,0:T(8,128)} custom-call(f32[128,8,128]{2,1,0:T(8,128)S(1)} %bitcast.11, f32[4,128,128]{2,1,0:T(8,128)S(1)} %get-tuple-element.8.tables), custom_call_target="tpu_custom_call" | custom-call | tf_op jit(solution)/shard_map/pallas_call | solution.py:536

commit v8 on v7

--- a/solution.py
+++ b/solution.py
@@ -391,8 +391,6 @@
     def lower_half(j):
         pl.when(~bottom)(lambda: deep_up(j).wait_recv())
         vertical(j, 4, 2)
-        for i in range(PART):
-            settled[x, j * PART + i] = mixed[x, j * PART + i]
 
     def follow(lead, lag):
         for j in range(lead):
@@ -406,12 +404,17 @@
                 forward(lead + j)
 
     corner = band < 2
-    together = (z > depth // 2) | (top & corner)
-    apart = ~together & ~((z == 1) & corner)
+    together = z > depth // 2
+    start = top & corner
+    next_corner = (z == 1) & corner
+    apart = ~together & ~start & ~next_corner
     pl.when(together)(lambda: follow(4, 1))
     pl.when(apart)(lambda: follow(6, 2))
-    pl.when(~together & ~apart)(lambda: follow(PIECES, 0))
-
+    pl.when(start)(lambda: follow(2, 0))
+    pl.when(next_corner)(lambda: follow(PIECES, 0))
+
+    for i in range(GROUP):
+        settled[x, i] = mixed[x, i]
     settle_bytes(settled.at[pl.ds(0, 3)], back_recv)
     settle_bytes(moved.at[pl.ds(1, 3)], ring_send)
     settle_bytes(mixed.at[pl.ds(0, 3)], back_send)

time: 24.9 us -> 25.5 us (1.024)
  Pallas kernels: 24.8 us -> 25.2 us
    pallas_call x1, Pallas kernels: 23.5 us -> 23.9 us  [local(): pl.pallas_call(functools.partial(step_kernel, depth, bands), out_shape=(j...]
where the time goes in v8:
time: 25.5 us; the launch traced here: 25.2 us
  Pallas kernels  25.2 us (99%)
    pallas_call x1, Pallas kernels, local(): pl.pallas_call(functools.partial(step_kernel, depth, bands), out_shape=(j...  23.9 us
    pallas_call x1, Pallas kernels, local(): pl.pallas_call(collide_kernel, out_shape=jax.ShapeDtypeStruct((NB,) + til...  1.22 us

profile of v8, /device:TPU:1, one launch (start us, length us, event | category | flops | bytes accessed | tf_op | source)
XLA Modules:
  0.0 25.2 jit_solution(10459744535300838793)
XLA Ops:
  0.0 23.9 %shard_map.91 = (f32[4,32,8,128]{3,2,1,0:T(8,128)S(1)}, f32[4,128,128]{2,1,0:T(8,128)S(1)}) custom-call(f32[128,8,128]{2,1,0:T(8,128)} %bitcast.12, f32[1,4,256]{2,1,0:T(4,128)} %vel_x_hbm.1, f32[1,4,256]{2,1,0:T(4,128)} %vel_y_hbm.1, s32[4,256]{1,0:T(4,128)} %sea_mask_hbm.1, f32[128]{0:T(128)} %settle_hbm.1, s32[128]{0:T(128)} %classes_hbm.1, f32[8]{0:T(128)} %up_hbm.1, ...), custom_call_target="tpu_custom_call" | custom-call | tf_op jit(solution)/shard_map/pallas_call | solution.py:494
  24.0 1.2 %shard_map.92 = f32[128,8,128]{2,1,0:T(8,128)} custom-call(f32[128,8,128]{2,1,0:T(8,128)S(1)} %bitcast.11, f32[4,128,128]{2,1,0:T(8,128)S(1)} %get-tuple-element.8.tables), custom_call_target="tpu_custom_call" | custom-call | tf_op jit(solution)/shard_map/pallas_call | solution.py:539
